TPU v7x, 32 devices: a whole 2x2x4 slice. The times are simulated.
32 devices in a mesh: section: 4 (over y, x), dp: 2 (over core), mp: 4 (over z).
Axes of the slice: x: 2, y: 2, z: 4, core: 2. Of those that a mesh axis runs over, the one named last changes fastest.
Arguments:
- act_sent: bfloat16 [4, 16, 3072], P('section', ('dp', 'mp')), may hold values from -6 to 6
- new_batch: bfloat16 [16, 3072], P(('dp', 'mp')), may hold values from -6 to 6
- saved_input: bfloat16 [4, 16, 3072], P('section', ('dp', 'mp')), may hold values from -6 to 6
- grad_sent: bfloat16 [4, 16, 3072], P('section', ('dp', 'mp')), may hold values from -6 to 6
- loss_grad: bfloat16 [16, 3072], P(('dp', 'mp')), may hold values from -6 to 6
- ln_gain: float32 [4, 3072], P('section'), may hold values from 0.1 to 1.9
- w_in: bfloat16 [4, 3072, 16384], P('section', None, 'mp'), may hold values from -0.109375 to 0.109375
- w_out: bfloat16 [4, 3072, 16384], P('section', None, 'mp'), may hold values from -0.046875 to 0.046875
Outputs:
- act_out: bfloat16 [4, 16, 3072], P('section', ('dp', 'mp'))
- grad_out: bfloat16 [4, 16, 3072], P('section', ('dp', 'mp'))
- grad_w_in: bfloat16 [4, 3072, 16384], P('section', 'dp', 'mp')
- grad_w_out: bfloat16 [4, 3072, 16384], P('section', 'dp', 'mp')
All inputs are finite; a program needn't handle non-finite values.
Results may differ from a plain program's by a relative error of at most 0.0075.
Values may be sent and summed in bfloat16 or wider, within the bound.
No kernel may reach another device: no remote copies, remote signals or barrier semaphores. Data moves between devices by JAX's collectives and lax.ppermute only.
A program may use at most 128 MiB of HBM per device.

v0:
```python
import jax
import jax.numpy as jnp
from jax import lax
from jax.sharding import PartitionSpec as P

gelu_c = 0.7978845608028654


def from_behind(block, axis, distance):
    devices = range(lax.axis_size(axis))
    route = [(i - distance, i) for i in devices if i - distance in devices]
    return lax.ppermute(block, axis, route)


def gelu_pair(h):
    inner = gelu_c * (h + 0.044715 * h * h * h)
    tval = jnp.tanh(inner)
    value = 0.5 * h * (1.0 + tval)
    slope = 0.5 * (1.0 + tval) + 0.5 * h * (1.0 - tval * tval) * gelu_c * (
        1.0 + 3.0 * 0.044715 * h * h
    )
    return (value, slope)


def normalize(rows):
    xval = rows.astype(jnp.float32)
    centre = xval - jnp.mean(xval, axis=-1, keepdims=True)
    rstd = lax.rsqrt(jnp.mean(centre * centre, axis=-1, keepdims=True) + 1e-05)
    return (centre * rstd, rstd)


def contract_rows(left, right):
    return lax.dot_general(
        left, right, (((0,), (0,)), ((), ())), preferred_element_type=jnp.float32
    )


def per_device(act_sent, new_batch, saved_input, grad_sent, loss_grad, ln_gain, w_in, w_out):
    section_idx = lax.axis_index("section")
    sections = lax.axis_size("section")
    arrived = from_behind(act_sent, "section", 1)
    returned = from_behind(grad_sent, "section", -1)
    x_fwd = jnp.where(section_idx == 0, new_batch, arrived[0])
    upstream = jnp.where(section_idx == sections - 1, loss_grad, returned[0])
    gain = ln_gain[0]
    nhat_fwd, _ = normalize(x_fwd)
    n_fwd = (nhat_fwd * gain).astype(jnp.bfloat16)
    nhat_bwd, rstd_bwd = normalize(saved_input[0])
    n_bwd = (nhat_bwd * gain).astype(jnp.bfloat16)
    rows_fwd, rows_bwd, rows_up = (
        lax.all_gather(n_fwd, "mp", axis=0, tiled=True),
        lax.all_gather(n_bwd, "mp", axis=0, tiled=True),
        lax.all_gather(upstream, "mp", axis=0, tiled=True),
    )
    weight_in = w_in[0]
    weight_out = w_out[0]
    h_fwd = jnp.dot(rows_fwd, weight_in, preferred_element_type=jnp.float32)
    g_fwd = gelu_pair(h_fwd)[0].astype(jnp.bfloat16)
    branch_part = lax.dot_general(
        g_fwd, weight_out, (((1,), (1,)), ((), ())), preferred_element_type=jnp.float32
    )
    h_bwd = jnp.dot(rows_bwd, weight_in, preferred_element_type=jnp.float32)
    g_val, slope = gelu_pair(h_bwd)
    g_bwd = g_val.astype(jnp.bfloat16)
    grad_act = jnp.dot(rows_up, weight_out, preferred_element_type=jnp.float32)
    grad_hidden = (grad_act * slope).astype(jnp.bfloat16)
    norm_part = lax.dot_general(
        grad_hidden, weight_in, (((1,), (1,)), ((), ())), preferred_element_type=jnp.float32
    )
    branch_sum, grad_norm = (
        lax.psum_scatter(branch_part, "mp", scatter_dimension=0, tiled=True),
        lax.psum_scatter(norm_part, "mp", scatter_dimension=0, tiled=True),
    )
    act_out = (x_fwd.astype(jnp.float32) + branch_sum).astype(jnp.bfloat16)
    scaled = grad_norm * gain
    grad_in = upstream.astype(jnp.float32) + rstd_bwd * (
        scaled
        - jnp.mean(scaled, axis=-1, keepdims=True)
        - nhat_bwd * jnp.mean(scaled * nhat_bwd, axis=-1, keepdims=True)
    )
    all_norm, all_up, all_act, all_hidden = (
        lax.all_gather(rows_bwd, "dp", axis=0, tiled=True),
        lax.all_gather(rows_up, "dp", axis=0, tiled=True),
        lax.all_gather(g_bwd, "dp", axis=0, tiled=True),
        lax.all_gather(grad_hidden, "dp", axis=0, tiled=True),
    )
    replicas = lax.axis_size("dp")
    half = weight_in.shape[0] // replicas
    start = lax.axis_index("dp") * half
    cols_norm = lax.dynamic_slice_in_dim(all_norm, start, half, 1)
    cols_up = lax.dynamic_slice_in_dim(all_up, start, half, 1)
    block = rows_bwd.shape[0]
    sum_in = jnp.zeros((half, weight_in.shape[1]), jnp.float32)
    sum_out = jnp.zeros((half, weight_in.shape[1]), jnp.float32)
    for replica in range(replicas):
        low = replica * block
        term_in = contract_rows(cols_norm[low : low + block], all_hidden[low : low + block])
        term_out = contract_rows(cols_up[low : low + block], all_act[low : low + block])
        sum_in = sum_in + term_in.astype(jnp.bfloat16).astype(jnp.float32)
        sum_out = sum_out + term_out.astype(jnp.bfloat16).astype(jnp.float32)
    return (
        act_out[None],
        grad_in.astype(jnp.bfloat16)[None],
        sum_in.astype(jnp.bfloat16)[None],
        sum_out.astype(jnp.bfloat16)[None],
    )


def solution(mesh):
    return jax.shard_map(
        per_device,
        mesh=mesh,
        in_specs=(
            P("section", ("dp", "mp"), None),
            P(("dp", "mp"), None),
            P("section", ("dp", "mp"), None),
            P("section", ("dp", "mp"), None),
            P(("dp", "mp"), None),
            P("section", None),
            P("section", None, "mp"),
            P("section", None, "mp"),
        ),
        out_specs=(
            P("section", ("dp", "mp"), None),
            P("section", ("dp", "mp"), None),
            P("section", "dp", "mp"),
            P("section", "dp", "mp"),
        ),
        check_vma=False,
    )
```

profile of v0, /device:TPU:0, one launch (start us, length us, event | category | flops | bytes accessed | tf_op | source)
XLA Modules:
  0.0 181.2 jit_solution(3140549871322711195)
XLA Ops:
  7.2 4.9 %collective-permute-start = (bf16[1,2,3072]{2,1,0:T(2,128)(2,1)}, bf16[1,2,3072]{2,1,0:T(2,128)(2,1)S(1)}, u32[]{:S(2)}, u32[]{:S(2)}) collective-permute-start(bf16[1,2,3072]{2,1,0:T(2,128)(2,1)} %param.8), channel_id=1, source_target_pairs={{0,8},{8,16},{16,24},{1,9},{9,17},{17,25},{2,10},{10,18},{18,26},{... | collective-permute-start | bytes 36872 | tf_op jit(solution)/shard_map/ppermute | solution.py:12
  12.1 1.3 collective-permute-start.1
  13.4 0.8 convert_reduce_fusion.1
  14.2 0.9 fusion.48
  15.2 1.2 dynamic-slice
  17.1 0.9 convert_reduce_fusion
  19.0 13.4 %all-gather.2 = bf16[4,2,3072]{2,1,0:T(2,128)(2,1)S(1)} all-gather(bf16[1,2,3072]{2,1,0:T(2,128)(2,1)S(1)} %get-tuple-element.10), channel_id=1, replica_groups=mesh['section'=4,'dp'=2,'mp'=4] {'mp'}, dimensions={0}, use_global_device_ids=true | all-gather | bytes 61440 | tf_op jit(solution)/shard_map/all_gather | solution.py:52
  32.4 13.1 %all-gather.1 = bf16[4,2,3072]{2,1,0:T(2,128)(2,1)S(1)} all-gather(bf16[1,2,3072]{2,1,0:T(2,128)(2,1)S(1)} %fusion.60), channel_id=1, replica_groups=mesh['section'=4,'dp'=2,'mp'=4] {'mp'}, dimensions={0}, use_global_device_ids=true | all-gather | bytes 61440 | tf_op jit(solution)/shard_map/all_gather | solution.py:53
  45.6 1.9 %all_gather.26 = bf16[16,3072]{1,0:T(8,128)(2,1)S(1)} all-gather(bf16[8,3072]{1,0:T(8,128)(2,1)S(1)} %reshape.44), channel_id=1, replica_groups=mesh['section'=4,'dp'=2,'mp'=4] {'dp'}, dimensions={0}, use_global_device_ids=true | all-gather | bytes 147456 | tf_op jit(solution)/shard_map/all_gather | solution.py:83
  47.4 1.9 %all_gather.24 = bf16[16,3072]{1,0:T(8,128)(2,1)S(1)} all-gather(bf16[8,3072]{1,0:T(8,128)(2,1)S(1)} %reshape.46), channel_id=1, replica_groups=mesh['section'=4,'dp'=2,'mp'=4] {'dp'}, dimensions={0}, use_global_device_ids=true | all-gather | bytes 147456 | tf_op jit(solution)/shard_map/all_gather | solution.py:82
  49.3 9.9 %multiply_convert_fusion = (bf16[8,4096]{1,0:T(8,128)(2,1)S(1)}, f32[8,4096]{1,0:T(8,128)S(1)}) fusion(bf16[8,3072]{1,0:T(8,128)(2,1)S(1)} %reshape.46, bf16[1,3072,4096]{2,1,0:T(8,128)(2,1)} %param.14), kind=kOutput, calls=%fused_computation.33 | convolution fusion | flops 201621504 | bytes 25411584 | tf_op jit(solution)/shard_map/dot_general | solution.py:62
  59.2 10.0 %fusion.15 = bf16[8,4096]{1,0:T(8,128)(2,1)S(1)} fusion(bf16[8,3072]{1,0:T(8,128)(2,1)S(1)} %reshape.44, bf16[1,3072,4096]{2,1,0:T(8,128)(2,1)} %param.15, f32[8,4096]{1,0:T(8,128)S(1)} %get-tuple-element.13), kind=kOutput, calls=%fused_computation.19 | convolution fusion | flops 201949184 | bytes 25411584 | tf_op jit(solution)/shard_map/dot_general | solution.py:65
  69.2 12.2 %fusion.4 = f32[8,3072]{1,0:T(8,128)} fusion(bf16[8,4096]{1,0:T(8,128)(2,1)S(1)} %fusion.15, bf16[1,3072,4096]{2,1,0:T(8,128)(2,1)} %param.14), kind=kOutput, calls=%fused_computation.4 | convolution fusion | flops 201326592 | bytes 25329664 | tf_op jit(solution)/shard_map/dot_general | solution.py:67
  81.4 1.9 %all_gather.25 = bf16[16,4096]{1,0:T(8,128)(2,1)S(1)} all-gather(bf16[8,4096]{1,0:T(8,128)(2,1)S(1)} %fusion.15), channel_id=1, replica_groups=mesh['section'=4,'dp'=2,'mp'=4] {'dp'}, dimensions={0}, use_global_device_ids=true | all-gather | bytes 196608 | tf_op jit(solution)/shard_map/all_gather | solution.py:85
  83.3 13.1 %all-gather = bf16[4,2,3072]{2,1,0:T(2,128)(2,1)S(1)} all-gather(bf16[1,2,3072]{2,1,0:T(2,128)(2,1)S(1)} %get-tuple-element.11), channel_id=1, replica_groups=mesh['section'=4,'dp'=2,'mp'=4] {'mp'}, dimensions={0}, use_global_device_ids=true | all-gather | bytes 61440 | tf_op jit(solution)/shard_map/all_gather | solution.py:51
  96.4 19.8 %fusion.2 = f32[8,3072]{1,0:T(8,128)} fusion(bf16[1,3072,4096]{2,1,0:T(8,128)(2,1)} %param.15, bf16[8,3072]{1,0:T(8,128)(2,1)S(1)} %reshape.42, bf16[1,3072,4096]{2,1,0:T(8,128)(2,1)} %param.14), kind=kOutput, calls=%fused_computation.2 | convolution fusion | flops 402948096 | bytes 50479104 | tf_op jit(solution)/shard_map/dot_general | solution.py:59
  116.1 2.1 %all_gather.27 = bf16[16,4096]{1,0:T(8,128)(2,1)S(1)} all-gather(bf16[8,4096]{1,0:T(8,128)(2,1)S(1)} %get-tuple-element.12), channel_id=1, replica_groups=mesh['section'=4,'dp'=2,'mp'=4] {'dp'}, dimensions={0}, use_global_device_ids=true | all-gather | bytes 196608 | tf_op jit(solution)/shard_map/all_gather | solution.py:84
  118.2 6.6 %convolution_convert_fusion.2 = bf16[1536,4096]{1,0:T(8,128)(2,1)} fusion(bf16[16,4096]{1,0:T(8,128)(2,1)S(1)} %all_gather.25, bf16[16,3072]{1,0:T(8,128)(2,1)S(1)} %all_gather.24, s32[]{:T(128)S(6)} %add.72, s32[]{:T(128)S(6)} %select_n.22), kind=kOutput, calls=%fused_computation.14 | convolution fusion | flops 106954752 | bytes 12673032 | tf_op jit(solution)/shard_map/dot_general | solution.py:33
  124.8 9.4 %fusion.10 = bf16[1,1536,4096]{2,1,0:T(8,128)(2,1)} fusion(bf16[1536,4096]{1,0:T(8,128)(2,1)} %convolution_convert_fusion.2, bf16[16,4096]{1,0:T(8,128)(2,1)S(1)} %all_gather.25, bf16[16,3072]{1,0:T(8,128)(2,1)S(1)} %all_gather.24, s32[]{:T(128)S(6)} %select_n.22), kind=kOutput, calls=%fused_computation.16 | convolution fusion | flops 132120576 | bytes 25255940 | tf_op jit(solution)/shard_map/dot_general | solution.py:33
  134.3 6.6 %convolution_convert_fusion = bf16[1536,4096]{1,0:T(8,128)(2,1)} fusion(bf16[16,4096]{1,0:T(8,128)(2,1)S(1)} %all_gather.27, bf16[16,3072]{1,0:T(8,128)(2,1)S(1)} %all_gather.26, s32[]{:T(128)S(6)} %add.72, s32[]{:T(128)S(6)} %select_n.22), kind=kOutput, calls=%fused_computation.12 | convolution fusion | flops 106954752 | bytes 12673032 | tf_op jit(solution)/shard_map/dot_general | solution.py:33
  140.9 9.4 %fusion.11 = bf16[1,1536,4096]{2,1,0:T(8,128)(2,1)} fusion(bf16[1536,4096]{1,0:T(8,128)(2,1)} %convolution_convert_fusion, bf16[16,4096]{1,0:T(8,128)(2,1)S(1)} %all_gather.27, bf16[16,3072]{1,0:T(8,128)(2,1)S(1)} %all_gather.26, s32[]{:T(128)S(6)} %select_n.22), kind=kOutput, calls=%fused_computation.17 | convolution fusion | flops 132120576 | bytes 25255940 | tf_op jit(solution)/shard_map/dot_general | solution.py:33
  150.3 21.2 %all-reduce.5.cloned.1.call-done = (f32[8,3072]{1,0:T(8,128)}, f32[8,3072]{1,0:T(8,128)}) async-done(((f32[8,3072]{1,0:T(8,128)}, f32[8,3072]{1,0:T(8,128)}), (f32[8,3072]{1,0:T(8,128)}, f32[8,3072]{1,0:T(8,128)})) %all-reduce.5.cloned.1.call-update) | async-done | bytes 196624
  171.6 1.1 fusion.65
  172.7 1.7 fusion.54
  (22 shorter events, 1.3 us)
Async XLA Ops:
  7.2 164.4 %all-reduce.5.cloned.1.call-start = ((), (), s32[]{:S(2)}) async-start(), calls=%async_computation | async-start | bytes 393216
  7.2 9.9 %collective-permute-start = (bf16[1,2,3072]{2,1,0:T(2,128)(2,1)}, bf16[1,2,3072]{2,1,0:T(2,128)(2,1)S(1)}, u32[]{:S(2)}, u32[]{:S(2)}) collective-permute-start(bf16[1,2,3072]{2,1,0:T(2,128)(2,1)} %param.8), channel_id=1, source_target_pairs={{0,8},{8,16},{16,24},{1,9},{9,17},{17,25},{2,10},{10,18},{18,26},{... | collective-permute-start | bytes 36872 | tf_op jit(solution)/shard_map/ppermute | solution.py:12
  12.1 20.3 %collective-permute-start.1 = (bf16[1,2,3072]{2,1,0:T(2,128)(2,1)}, bf16[1,2,3072]{2,1,0:T(2,128)(2,1)S(1)}, u32[]{:S(2)}, u32[]{:S(2)}) collective-permute-start(bf16[1,2,3072]{2,1,0:T(2,128)(2,1)} %param.11), channel_id=1, source_target_pairs={{8,0},{16,8},{24,16},{9,1},{17,9},{25,17},{10,2},{18,10},{26,18},{... | collective-permute-start | bytes 36872 | tf_op jit(solution)/shard_map/ppermute | solution.py:12
  134.2 37.3 %copy-start = (bf16[1,2,3072]{2,1,0:T(2,128)(2,1)S(1)}, bf16[1,2,3072]{2,1,0:T(2,128)(2,1)}, u32[]{:S(2)}) copy-start(bf16[1,2,3072]{2,1,0:T(2,128)(2,1)} %param.10) | copy-start | bytes 36868
  134.2 37.3 %copy-start.1 = (f32[1,3072]{1,0:T(1,128)S(1)}, f32[1,3072]{1,0:T(1,128)}, u32[]{:S(2)}) copy-start(f32[1,3072]{1,0:T(1,128)} %param.13) | copy-start | bytes 36868
  134.3 38.4 %copy-start.2 = (bf16[2,3072]{1,0:T(2,128)(2,1)S(1)}, bf16[2,3072]{1,0:T(2,128)(2,1)}, u32[]{:S(2)}) copy-start(bf16[2,3072]{1,0:T(2,128)(2,1)} %param.12) | copy-start | bytes 36868
Sparse Core Ops, SparseCore 0:
  134.4 37.1 all-reduce.4
where the time goes:
time: 182 us; the launch traced here: 181 us
  matrix products  83.9 us (46%)
  blocking collectives  47.2 us (26%)
  waiting for transfers between devices  21.2 us (12%)
  between operations  14.8 us (8%)
  other arithmetic  6.5 us (4%)
  starting transfers between devices  6.2 us (3%)
    dot_general x4, matrix products, contract_rows(): lax.dot_general(left, right, (((0,), (0,)), ((), ())), preferred_element_...  32.1 us
    unnamed x2, waiting for transfers between devices  21.2 us
    dot_general x1, matrix products, per_device(): lax.dot_general(g_fwd, weight_out, (((1,), (1,)), ((), ())), preferred_el...  19.8 us
    all_gather x1, blocking collectives, per_device(): lax.all_gather(n_bwd, 'mp', axis=0, tiled=True)  13.4 us
    all_gather x1, blocking collectives, per_device(): lax.all_gather(upstream, 'mp', axis=0, tiled=True)  13.1 us
    all_gather x1, blocking collectives, per_device(): lax.all_gather(n_fwd, 'mp', axis=0, tiled=True)  13.1 us
    dot_general x1, matrix products, per_device(): lax.dot_general(grad_hidden, weight_in, (((1,), (1,)), ((), ())), preferr...  12.2 us
    dot_general x1, matrix products, per_device(): grad_act = jnp.dot(rows_up, weight_out, preferred_element_type=jnp.float32)  10 us
  transfers between devices with their start and end apart: 3, of which 1 were waited for; matrix products, arithmetic and copies ran while one was open for 12% of the time, Pallas kernels for 0%

commit v1 on v0

v1 whole, which is shorter than its diff:
```python
import functools

import jax
import jax.numpy as jnp
from jax import lax
from jax.experimental import pallas as pl
from jax.experimental.pallas import tpu as pltpu
from jax.sharding import PartitionSpec as P

GELU_C = 0.7978845608028654
BF16 = jnp.bfloat16
F32 = jnp.float32
MIB = 1 << 20


def gelu_value(h):
    tval = jnp.tanh(GELU_C * (h + 0.044715 * h * h * h))
    return 0.5 * h * (1.0 + tval)


def gelu_pair(h):
    tval = jnp.tanh(GELU_C * (h + 0.044715 * h * h * h))
    value = 0.5 * h * (1.0 + tval)
    slope = 0.5 * (1.0 + tval) + 0.5 * h * (1.0 - tval * tval) * GELU_C * (
        1.0 + 3.0 * 0.044715 * h * h
    )
    return value, slope


def normalize(xval):
    centre = xval - jnp.mean(xval, axis=-1, keepdims=True)
    rstd = lax.rsqrt(jnp.mean(centre * centre, axis=-1, keepdims=True) + 1e-05)
    return centre * rstd, rstd


def contract_last(left, right):
    return lax.dot_general(
        left, right, (((1,), (1,)), ((), ())), preferred_element_type=F32
    )


def contract_first(left, right):
    return lax.dot_general(
        left, right, (((0,), (0,)), ((), ())), preferred_element_type=F32
    )


def block_kernel(sections, dp, chunks, where_ref, *refs):
    rows_refs = refs[:dp]
    gain_ref, win_hbm, wout_hbm = refs[dp : dp + 3]
    hid_ref, part_ref, norm_ref, up_ref = refs[dp + 3 : dp + 7]
    both, win, wout, branch, dnorm, sem_in, sem_out = refs[dp + 7 :]
    section, replica = where_ref[0], where_ref[1]
    block = rows_refs[0].shape[1]
    tokens = dp * block
    hidden = win.shape[1]
    width = hidden // chunks
    start = replica * hidden

    def fetch(source, target, sem, chunk):
        columns = pl.ds(pl.multiple_of(start + chunk * width, width), width)
        return pltpu.make_async_copy(
            source.at[:, columns], target.at[:, pl.ds(chunk * width, width)], sem.at[chunk]
        )

    for chunk in range(chunks):
        fetch(win_hbm, win, sem_in, chunk).start()
        fetch(wout_hbm, wout, sem_out, chunk).start()

    behind = lax.rem(section + sections - 1, sections)
    ahead = lax.rem(section + 1, sections)
    gain = gain_ref[...]

    def rows_of(slot, owner):
        rows = rows_refs[0][slot]
        for k in range(1, dp):
            rows = jnp.where(
                lax.rem(replica + dp - k, dp) == owner, rows_refs[k][slot], rows
            )
        return rows

    for owner in range(dp):
        low = owner * block
        nhat, _ = normalize(rows_of(behind, owner).astype(F32))
        both[low : low + block, :] = (nhat * gain).astype(BF16)
        nhat, _ = normalize(rows_of(section, owner).astype(F32))
        n_bwd = (nhat * gain).astype(BF16)
        both[tokens + low : tokens + low + block, :] = n_bwd
        norm_ref[low : low + block, :] = n_bwd
        up_ref[low : low + block, :] = rows_of(ahead, owner)

    def first(chunk):
        columns = slice(chunk * width, (chunk + 1) * width)
        fetch(win_hbm, win, sem_in, chunk).wait()
        h = jnp.dot(both[...], win[:, columns], preferred_element_type=F32)
        fetch(wout_hbm, wout, sem_out, chunk).wait()
        grad_act = jnp.dot(up_ref[...], wout[:, columns], preferred_element_type=F32)
        g_fwd = gelu_value(h[:tokens]).astype(BF16)
        g_bwd, slope = gelu_pair(h[tokens:])
        dh = (grad_act * slope).astype(BF16)
        hid_ref[0, :, columns] = dh
        hid_ref[1, :, columns] = g_bwd.astype(BF16)
        return g_fwd, dh

    def second(chunk, g_fwd, dh):
        columns = slice(chunk * width, (chunk + 1) * width)
        term_n = contract_last(dh, win[:, columns])
        term_b = contract_last(g_fwd, wout[:, columns])
        if chunk == 0:
            dnorm[...] = term_n
            branch[...] = term_b
        else:
            dnorm[...] += term_n
            branch[...] += term_b

    pending = first(0)
    for chunk in range(1, chunks):
        later = first(chunk)
        second(chunk - 1, *pending)
        pending = later
    second(chunks - 1, *pending)

    owners, mine = part_ref.shape[0], part_ref.shape[1] // 2
    for owner in range(owners):
        rows = slice(owner * mine, (owner + 1) * mine)
        part_ref[owner, :mine, :] = branch[rows, :].astype(BF16)
        part_ref[owner, mine:, :] = dnorm[rows, :].astype(BF16)


def weight_kernel(where_ref, norm_ref, up_ref, hid_ref, *refs):
    in_ref, out_ref = refs[-2:]
    in_ref[...] = contract_first(norm_ref[...], hid_ref[0]).astype(BF16)
    out_ref[...] = contract_first(up_ref[...], hid_ref[1]).astype(BF16)


def finish_kernel(sections, mp, where_ref, recv_ref, rows_ref, saved_ref, gain_ref, act_ref, grad_ref):
    section, lane = where_ref[0], where_ref[2]
    mine = saved_ref.shape[1]
    total = jnp.sum(recv_ref[...].astype(F32), axis=0)
    behind = lax.rem(section + sections - 1, sections) * mp + lane
    ahead = lax.rem(section + 1, sections) * mp + lane
    act_ref[0] = (rows_ref[behind].astype(F32) + total[:mine]).astype(BF16)
    nhat, rstd = normalize(saved_ref[0].astype(F32))
    scaled = total[mine:] * gain_ref[...]
    grad = rows_ref[ahead].astype(F32) + rstd * (
        scaled
        - jnp.mean(scaled, axis=-1, keepdims=True)
        - nhat * jnp.mean(scaled * nhat, axis=-1, keepdims=True)
    )
    grad_ref[0] = grad.astype(BF16)


def divisor(size, most):
    return max(k for k in range(1, most + 1) if size % k == 0)


def per_device(sections, dp, mp, act_sent, new_batch, saved_input, grad_sent, loss_grad, ln_gain, w_in, w_out):
    section = lax.axis_index("section")
    replica = lax.axis_index("dp")
    lane = lax.axis_index("mp")
    where = jnp.stack([section, replica, lane]).astype(jnp.int32)
    mine, width = new_batch.shape
    hidden = w_in.shape[2] // dp
    block = mp * mine
    tokens = dp * block
    vmem = pl.BlockSpec(memory_space=pltpu.VMEM)
    smem = pl.BlockSpec(memory_space=pltpu.SMEM)
    hbm = pl.BlockSpec(memory_space=pl.ANY)

    to_next = jnp.where(section == sections - 1, new_batch, act_sent[0])
    to_last = jnp.where(section == 0, loss_grad, grad_sent[0])
    step = ((jnp.arange(sections) - section) % sections)[:, None, None, None]
    sent = jnp.where(step == 0, saved_input[0], jnp.where(step == 1, to_next, to_last))
    sent = jnp.broadcast_to(sent, (sections, mp, mine, width)).reshape(sections * mp, mine, width)
    got = lax.all_to_all(sent, ("section", "mp"), 0, 0)
    own = got.reshape(sections, block, width)
    rows = [own] + [
        lax.ppermute(own, "dp", [(i, (i + k) % dp) for i in range(dp)]) for k in range(1, dp)
    ]

    chunks = divisor(hidden // 128, 4)
    hid, part, n_bwd, upstream = pl.pallas_call(
        functools.partial(block_kernel, sections, dp, chunks),
        in_specs=[smem] + [vmem] * dp + [vmem, hbm, hbm],
        out_specs=[vmem] * 4,
        out_shape=[
            jax.ShapeDtypeStruct((2, tokens, hidden), BF16),
            jax.ShapeDtypeStruct((dp * mp, 2 * mine, width), BF16),
            jax.ShapeDtypeStruct((tokens, width), BF16),
            jax.ShapeDtypeStruct((tokens, width), BF16),
        ],
        scratch_shapes=[
            pltpu.VMEM((2 * tokens, width), BF16),
            pltpu.VMEM((width, hidden), BF16),
            pltpu.VMEM((width, hidden), BF16),
            pltpu.VMEM((tokens, width), F32),
            pltpu.VMEM((tokens, width), F32),
            pltpu.SemaphoreType.DMA((chunks,)),
            pltpu.SemaphoreType.DMA((chunks,)),
        ],
        compiler_params=pltpu.CompilerParams(vmem_limit_bytes=44 * MIB),
        cost_estimate=pl.CostEstimate(
            flops=12 * tokens * width * hidden, bytes_accessed=4 * width * hidden, transcendentals=2 * tokens * hidden
        ),
        name="block",
    )(where, *rows, ln_gain, w_in[0], w_out[0])

    hids = [hid] + [
        lax.ppermute(hid, "dp", [(i, (i + k) % dp) for i in range(dp)]) for k in range(1, dp)
    ]
    recv = lax.all_to_all(part, ("dp", "mp"), 0, 0)

    half = width // dp
    tile = 128 * divisor(half // 128, max(1, 6 * 2048 // hidden))
    steps = half // tile
    grads = []
    for k in range(dp):
        grads = pl.pallas_call(
            weight_kernel,
            grid_spec=pltpu.PrefetchScalarGridSpec(
                num_scalar_prefetch=1,
                grid=(steps,),
                in_specs=[
                    pl.BlockSpec((tokens, tile), lambda i, w: (0, w[1] * steps + i)),
                    pl.BlockSpec((tokens, tile), lambda i, w: (0, w[1] * steps + i)),
                    pl.BlockSpec((2, tokens, hidden), lambda i, w: (0, 0, 0)),
                ]
                + [hbm] * len(grads),
                out_specs=[
                    pl.BlockSpec((tile, hidden), lambda i, w, k=k: (i, lax.rem(w[1] + dp - k, dp)))
                ]
                * 2,
            ),
            out_shape=[jax.ShapeDtypeStruct((half, dp * hidden), BF16)] * 2,
            input_output_aliases={4: 0, 5: 1} if grads else {},
            compiler_params=pltpu.CompilerParams(vmem_limit_bytes=32 * MIB),
            cost_estimate=pl.CostEstimate(
                flops=4 * tokens * half * hidden, bytes_accessed=4 * half * hidden, transcendentals=0
            ),
            name="weight",
        )(where, n_bwd, upstream, hids[k], *grads)

    act_out, grad_out = pl.pallas_call(
        functools.partial(finish_kernel, sections, mp),
        in_specs=[smem] + [vmem] * 4,
        out_specs=[vmem] * 2,
        out_shape=[jax.ShapeDtypeStruct((1, mine, width), BF16)] * 2,
        compiler_params=pltpu.CompilerParams(vmem_limit_bytes=16 * MIB),
        name="finish",
    )(where, recv, got, saved_input, ln_gain)
    return act_out, grad_out, grads[0][None], grads[1][None]


def solution(mesh):
    sizes = dict(mesh.shape)
    body = functools.partial(per_device, sizes["section"], sizes["dp"], sizes["mp"])
    return jax.shard_map(
        body,
        mesh=mesh,
        in_specs=(
            P("section", ("dp", "mp"), None),
            P(("dp", "mp"), None),
            P("section", ("dp", "mp"), None),
            P("section", ("dp", "mp"), None),
            P(("dp", "mp"), None),
            P("section", None),
            P("section", None, "mp"),
            P("section", None, "mp"),
        ),
        out_specs=(
            P("section", ("dp", "mp"), None),
            P("section", ("dp", "mp"), None),
            P("section", "dp", "mp"),
            P("section", "dp", "mp"),
        ),
        check_vma=False,
    )
```

time: 182 us -> 55.7 us (0.31)
  matrix products: 83.9 us -> 0 us
  blocking collectives: 47.2 us -> 17.3 us
  Pallas kernels: 0 us -> 29.3 us
  waiting for transfers between devices: 21.2 us -> 1.35 us
  between operations: 14.8 us -> 0.7 us
  other arithmetic: 6.5 us -> 1.7 us
  starting transfers between devices: 6.2 us -> 3.9 us
    dot_general x8 -> x0, matrix products: 83.9 us -> none  [the longest x4 32.1 us: contract_rows(): lax.dot_general(left, right, (((0,), (0,)), ((), ())), preferred_element_...]
    all_gather x7 -> x0, blocking collectives: 47.2 us -> none  [the longest x1 13.4 us: per_device(): lax.all_gather(n_bwd, 'mp', axis=0, tiled=True)]
    pallas_call x0 -> x4, Pallas kernels: none -> 29.3 us  [the longest x1 15.2 us: per_device(): pl.pallas_call(functools.partial(block_kernel, sections, dp, chunks), in_...]
    unnamed x2 -> x0, waiting for transfers between devices: 21.2 us -> none
    all_to_all x0 -> x1, blocking collectives: none -> 17.3 us  [per_device(): got = lax.all_to_all(sent, ('section', 'mp'), 0, 0)]
    ppermute x2, starting transfers between devices: 6.16 us -> 0.5 us  [the longest x1 0.42 us: per_device(): lax.ppermute(hid, 'dp', [(i, (i + k) % dp) for i in range(dp)])]
    reduce_sum x5 -> x0, other arithmetic: 3.96 us -> none  [the longest x2 1.7 us: normalize(): centre = xval - jnp.mean(xval, axis=-1, keepdims=True)]
    all_to_all x0 -> x1, starting transfers between devices: none -> 3.4 us  [per_device(): recv = lax.all_to_all(part, ('dp', 'mp'), 0, 0)]
  transfers between devices with their start and end apart: 3 -> 3, of which waited for: 1 -> 1; matrix products, arithmetic and copies ran while one was open for 12% -> 0% of each run, Pallas kernels for 0% -> 23%
where the time goes in v1:
time: 55.7 us; the launch traced here: 55.2 us
  Pallas kernels  29.3 us (53%)
  blocking collectives  17.3 us (31%)
  starting transfers between devices  3.9 us (7%)
  other arithmetic  1.7 us (3%)
  waiting for transfers between devices  1.35 us (2%)
  local copies, waits for them, and re-layouts  0.89 us (2%)
  between operations  0.7 us (1%)
    all_to_all x1, blocking collectives, per_device(): got = lax.all_to_all(sent, ('section', 'mp'), 0, 0)  17.3 us
    pallas_call x1, Pallas kernels, per_device(): pl.pallas_call(functools.partial(block_kernel, sections, dp, chunks), in_...  15.2 us
    pallas_call x2, Pallas kernels, per_device(): pl.pallas_call(weight_kernel, grid_spec=pltpu.PrefetchScalarGridSpec(num_...  12.6 us
    all_to_all x1, starting transfers between devices, per_device(): recv = lax.all_to_all(part, ('dp', 'mp'), 0, 0)  3.4 us
    pallas_call x1, Pallas kernels, per_device(): pl.pallas_call(functools.partial(finish_kernel, sections, mp), in_specs=[...  1.51 us
    ppermute x1, waiting for transfers between devices, per_device(): lax.ppermute(own, 'dp', [(i, (i + k) % dp) for i in range(dp)])  1.35 us
  transfers between devices with their start and end apart: 3, of which 1 were waited for; matrix products, arithmetic and copies ran while one was open for 0% of the time, Pallas kernels for 23%

profile of v1, /device:TPU:0, one launch (start us, length us, event | category | flops | bytes accessed | tf_op | source)
XLA Modules:
  0.0 55.2 jit_solution(7469122813007523543)
XLA Ops:
  0.7 0.8 %broadcast_select_fusion.2 = (bf16[2,3072]{1,0:T(2,128)(2,1)S(1)}, bf16[2,3072]{1,0:T(2,128)(2,1)S(1)}) fusion(bf16[2,3072]{1,0:T(2,128)(2,1)} %param.12, pred[]{:T(512)S(6)} %eq.27, bf16[1,2,3072]{2,1,0:T(2,128)(2,1)} %param.11, bf16[2,3072]{1,0:T(2,128)(2,1)} %param.9, bf16[1,2,3072]{2,1,0:T(2,128)(2,1)} %param.8, pred[]{:T(512)S(6)} %eq.26), kind=kLoop, calls=%fused_computation.2 | loop fusion | flops 12288 | bytes 73730 | tf_op jit(solution)/shard_map/jit(_where)/select_n | solution.py:171
  1.4 0.8 %broadcast_select_fusion = bf16[4,2,3072]{2,1,0:T(2,128)(2,1)S(1)} fusion(pred[4]{0:T(512)(128)(4,1)S(1)} %get-tuple-element.25, pred[4]{0:T(512)(128)(4,1)S(1)} %get-tuple-element.24, bf16[2,3072]{1,0:T(2,128)(2,1)S(1)} %get-tuple-element.26, bf16[2,3072]{1,0:T(2,128)(2,1)S(1)} %get-tuple-element.27, bf16[2,3072]{1,0:T(2,128)(2,1)} %bitcast.13), kind=kLoop, calls=%fused_computation | loop fusion | flops 49152 | bytes 86024 | tf_op jit(solution)/shard_map/jit(_where)/select_n | solution.py:173
  2.3 0.1 broadcast_in_dim.45
  2.4 17.3 %all_to_all.10.rows_ref = bf16[16,2,3072]{2,1,0:T(2,128)(2,1)S(1)} all-to-all(bf16[16,2,3072]{2,1,0:T(2,128)(2,1)S(1)} %bitcast.18), channel_id=1, replica_groups=mesh['section'=4,'dp'=2,'mp'=4] {'section','mp'}, dimensions={0} | all-to-all | bytes 393216 | tf_op jit(solution)/shard_map/all_to_all | solution.py:175
  19.7 0.1 reshape.44.refs_0_
  19.8 0.1 collective-permute-start
  19.9 0.1 pad_add_fusion.where_ref
  19.9 1.3 %collective-permute-done.refs_1_ = bf16[4,8,3072]{2,1,0:T(8,128)(2,1)S(1)} collective-permute-done((bf16[4,8,3072]{2,1,0:T(8,128)(2,1)S(1)}, bf16[4,8,3072]{2,1,0:T(8,128)(2,1)S(1)}, u32[]{:S(2)}, u32[]{:S(2)}) %collective-permute-start) | collective-permute-done | bytes 196640 | tf_op jit(solution)/shard_map/ppermute | solution.py:178
  21.3 0.0 copy-start
  21.3 0.7 %copy-done = f32[1,3072]{1,0:T(1,128)S(1)} copy-done((f32[1,3072]{1,0:T(1,128)S(1)}, f32[1,3072]{1,0:T(1,128)}, u32[]{:S(2)}) %copy-start) | copy-done | bytes 12312
  22.0 15.2 %block.1 = (bf16[2,16,2048]{2,1,0:T(8,128)(2,1)S(1)}, bf16[8,4,3072]{2,1,0:T(4,128)(2,1)}, bf16[16,3072]{1,0:T(8,128)(2,1)S(1)}, bf16[16,3072]{1,0:T(8,128)(2,1)S(1)}) custom-call(s32[3]{0:T(128)S(1)} %pad_add_fusion.where_ref, bf16[4,8,3072]{2,1,0:T(8,128)(2,1)S(1)} %reshape.44.refs_0_, bf16[4,8,3072]{2,1,0:T(8,128)(2,1)S(1)} %collective-permute-done.refs_1_, ...), custom_call_target="tpu_custom_call" | custom-call | flops 1207959552 | bytes 25165824 | tf_op jit(solution)/shard_map/block/pallas_call | solution.py:182
  37.2 3.4 %all-to-all-start.1 = ((bf16[8,4,3072]{2,1,0:T(4,128)(2,1)}), bf16[8,4,3072]{2,1,0:T(4,128)(2,1)S(1)}, u32[]{:S(2)}, u32[]{:S(2)}) async-start(bf16[8,4,3072]{2,1,0:T(4,128)(2,1)} %get-tuple-element.14), calls=%async_computation.1 | async-start | bytes 393216 | tf_op jit(solution)/shard_map/all_to_all | solution.py:211
  40.6 0.4 collective-permute-start.1
  41.0 6.3 %weight.2 = (bf16[1536,4096]{1,0:T(8,128)(2,1)}, bf16[1536,4096]{1,0:T(8,128)(2,1)}) custom-call(s32[3]{0:T(128)S(1)} %pad_add_fusion.where_ref, bf16[16,3072]{1,0:T(8,128)(2,1)S(1)} %get-tuple-element.17.norm_ref, bf16[16,3072]{1,0:T(8,128)(2,1)S(1)} %get-tuple-element.18.up_ref, bf16[2,16,2048]{2,1,0:T(8,128)(2,1)S(1)} %get-tuple-element.19.hid_ref), custom_call_target="tpu_custom_call" | custom-call | flops 201326592 | bytes 12582912 | tf_op jit(solution)/shard_map/weight/pallas_call | solution.py:218
  47.3 0.0 collective-permute-done.1.hid_ref
  47.3 0.0 copy-start.1
  47.3 0.0 copy-start.2
  47.3 6.3 %weight.3 = (bf16[1536,4096]{1,0:T(8,128)(2,1)}, bf16[1536,4096]{1,0:T(8,128)(2,1)}) custom-call(s32[3]{0:T(128)S(1)} %pad_add_fusion.where_ref, bf16[16,3072]{1,0:T(8,128)(2,1)S(1)} %get-tuple-element.17.norm_ref, bf16[16,3072]{1,0:T(8,128)(2,1)S(1)} %get-tuple-element.18.up_ref, ...), custom_call_target="tpu_custom_call", output_to_operand_aliasing={{0}: (4, {}), {1}: (5, {})} | custom-call | flops 201326592 | bytes 12582912 | tf_op jit(solution)/shard_map/weight/pallas_call | solution.py:218
  53.6 0.0 all-to-all-done.1.recv_ref
  53.6 0.0 copy-done.1
  53.6 0.0 copy-done.2
  53.6 1.5 %finish.1 = (bf16[1,2,3072]{2,1,0:T(2,128)(2,1)}, bf16[1,2,3072]{2,1,0:T(2,128)(2,1)}) custom-call(s32[3]{0:T(128)S(1)} %pad_add_fusion.where_ref, bf16[8,4,3072]{2,1,0:T(4,128)(2,1)S(1)} %all-to-all-done.1.recv_ref, bf16[16,2,3072]{2,1,0:T(2,128)(2,1)S(1)} %all_to_all.10.rows_ref, bf16[1,2,3072]{2,1,0:T(2,128)(2,1)S(1)} %copy-done.2, f32[1,3072]{1,0:T(1,128)S(1)} %copy-done.1), custom_call_target="tpu_custom_call" | custom-call | tf_op jit(solution)/shard_map/finish/pallas_call | solution.py:243
  (1 shorter events, 0.0 us)
Async XLA Ops:
  19.8 1.5 %collective-permute-start = (bf16[4,8,3072]{2,1,0:T(8,128)(2,1)S(1)}, bf16[4,8,3072]{2,1,0:T(8,128)(2,1)S(1)}, u32[]{:S(2)}, u32[]{:S(2)}) collective-permute-start(bf16[4,8,3072]{2,1,0:T(8,128)(2,1)S(1)} %reshape.44.refs_0_), channel_id=1, source_target_pairs={{0,4},{4,0},{1,5},{5,1},{2,6},{6,2},{3,7},{7,3},{8,12},{12,8},{9,1... | collective-permute-start | bytes 589832 | tf_op jit(solution)/shard_map/ppermute | solution.py:178
  21.3 0.7 %copy-start = (f32[1,3072]{1,0:T(1,128)S(1)}, f32[1,3072]{1,0:T(1,128)}, u32[]{:S(2)}) copy-start(f32[1,3072]{1,0:T(1,128)} %gain_ref.1) | copy-start | bytes 36868
  37.2 16.5 %all-to-all-start.1 = ((bf16[8,4,3072]{2,1,0:T(4,128)(2,1)}), bf16[8,4,3072]{2,1,0:T(4,128)(2,1)S(1)}, u32[]{:S(2)}, u32[]{:S(2)}) async-start(bf16[8,4,3072]{2,1,0:T(4,128)(2,1)} %get-tuple-element.14), calls=%async_computation.1 | async-start | bytes 393216 | tf_op jit(solution)/shard_map/all_to_all | solution.py:211
  40.6 6.7 %collective-permute-start.1 = (bf16[2,16,2048]{2,1,0:T(8,128)(2,1)S(1)}, bf16[2,16,2048]{2,1,0:T(8,128)(2,1)S(1)}, u32[]{:S(2)}, u32[]{:S(2)}) collective-permute-start(bf16[2,16,2048]{2,1,0:T(8,128)(2,1)S(1)} %get-tuple-element.19.hid_ref), channel_id=1, source_target_pairs={{0,4},{4,0},{1,5},{5,1},{2,6},{6,2},{3,7},{7,3},{8,12},{12,8},{9,1... | collective-permute-start | bytes 393224 | tf_op jit(solution)/shard_map/ppermute | solution.py:209
  47.3 6.3 %copy-start.1 = (f32[1,3072]{1,0:T(1,128)S(1)}, f32[1,3072]{1,0:T(1,128)}, u32[]{:S(2)}) copy-start(f32[1,3072]{1,0:T(1,128)} %gain_ref.1) | copy-start | bytes 36868
  47.3 6.3 %copy-start.2 = (bf16[1,2,3072]{2,1,0:T(2,128)(2,1)S(1)}, bf16[1,2,3072]{2,1,0:T(2,128)(2,1)}, u32[]{:S(2)}) copy-start(bf16[1,2,3072]{2,1,0:T(2,128)(2,1)} %saved_ref.1) | copy-start | bytes 36868

commit v2 on v1

--- a/solution.py
+++ b/solution.py
@@ -7,6 +7,7 @@
 from jax.experimental.pallas import tpu as pltpu
 from jax.sharding import PartitionSpec as P
 
+
 GELU_C = 0.7978845608028654
 BF16 = jnp.bfloat16
 F32 = jnp.float32
@@ -45,11 +46,46 @@
     )
 
 
-def block_kernel(sections, dp, chunks, where_ref, *refs):
+def send_kernel(sections, mp, where_ref, act_ref, batch_ref, saved_ref, grad_ref, loss_ref, sent_ref, sems):
+    section = where_ref[0]
+    behind = lax.rem(section + sections - 1, sections)
+    ahead = lax.rem(section + 1, sections)
+
+    def spread(source, target, sem):
+        def start(lane, carry):
+            pltpu.make_async_copy(source, sent_ref.at[target * mp + lane], sems.at[sem]).start()
+            return carry
+
+        lax.fori_loop(0, mp, start, 0, unroll=mp <= 8)
+
+    spread(saved_ref.at[0], section, 0)
+
+    @pl.when(section == sections - 1)
+    def _():
+        spread(batch_ref, ahead, 1)
+
+    @pl.when(section != sections - 1)
+    def _():
+        spread(act_ref.at[0], ahead, 1)
+
+    @pl.when(section == 0)
+    def _():
+        spread(loss_ref, behind, 2)
+
+    @pl.when(section != 0)
+    def _():
+        spread(grad_ref.at[0], behind, 2)
+
+    for sem in range(3):
+        whole = sent_ref.at[pl.ds(0, mp)]
+        pltpu.make_async_copy(whole, whole, sems.at[sem]).wait()
+
+
+def block_kernel(sections, dp, chunks, depth, where_ref, *refs):
     rows_refs = refs[:dp]
-    gain_ref, win_hbm, wout_hbm = refs[dp : dp + 3]
+    gain_hbm, win_hbm, wout_hbm = refs[dp : dp + 3]
     hid_ref, part_ref, norm_ref, up_ref = refs[dp + 3 : dp + 7]
-    both, win, wout, branch, dnorm, sem_in, sem_out = refs[dp + 7 :]
+    both, gain_ref, win, wout, branch, dnorm, sem_gain, sem_in, sem_out = refs[dp + 7 :]
     section, replica = where_ref[0], where_ref[1]
     block = rows_refs[0].shape[1]
     tokens = dp * block
@@ -57,18 +93,23 @@
     width = hidden // chunks
     start = replica * hidden
 
-    def fetch(source, target, sem, chunk):
-        columns = pl.ds(pl.multiple_of(start + chunk * width, width), width)
-        return pltpu.make_async_copy(
-            source.at[:, columns], target.at[:, pl.ds(chunk * width, width)], sem.at[chunk]
+    def fetch(chunk):
+        source = pl.ds(pl.multiple_of(start + chunk * width, 128), width)
+        target = pl.ds(chunk * width, width)
+        return (
+            pltpu.make_async_copy(win_hbm.at[:, source], win.at[:, target], sem_in.at[chunk]),
+            pltpu.make_async_copy(wout_hbm.at[:, source], wout.at[:, target], sem_out.at[chunk]),
         )
 
-    for chunk in range(chunks):
-        fetch(win_hbm, win, sem_in, chunk).start()
-        fetch(wout_hbm, wout, sem_out, chunk).start()
+    fetch_gain = pltpu.make_async_copy(gain_hbm, gain_ref, sem_gain)
+    fetch_gain.start()
+    for chunk in range(min(depth, chunks)):
+        for copy in fetch(chunk):
+            copy.start()
 
     behind = lax.rem(section + sections - 1, sections)
     ahead = lax.rem(section + 1, sections)
+    fetch_gain.wait()
     gain = gain_ref[...]
 
     def rows_of(slot, owner):
@@ -91,9 +132,12 @@
 
     def first(chunk):
         columns = slice(chunk * width, (chunk + 1) * width)
-        fetch(win_hbm, win, sem_in, chunk).wait()
+        for copy in fetch(chunk):
+            copy.wait()
+        if chunk + depth < chunks:
+            for copy in fetch(chunk + depth):
+                copy.start()
         h = jnp.dot(both[...], win[:, columns], preferred_element_type=F32)
-        fetch(wout_hbm, wout, sem_out, chunk).wait()
         grad_act = jnp.dot(up_ref[...], wout[:, columns], preferred_element_type=F32)
         g_fwd = gelu_value(h[:tokens]).astype(BF16)
         g_bwd, slope = gelu_pair(h[tokens:])
@@ -127,10 +171,29 @@
         part_ref[owner, mine:, :] = dnorm[rows, :].astype(BF16)
 
 
-def weight_kernel(where_ref, norm_ref, up_ref, hid_ref, *refs):
-    in_ref, out_ref = refs[-2:]
-    in_ref[...] = contract_first(norm_ref[...], hid_ref[0]).astype(BF16)
-    out_ref[...] = contract_first(up_ref[...], hid_ref[1]).astype(BF16)
+def weight_kernel(dp, tile, where_ref, norm_ref, up_ref, *refs):
+    hid_refs = refs[:dp]
+    targets, buffers, sems = refs[dp : dp + 2], refs[dp + 2 : dp + 4], refs[dp + 4]
+    replica = where_ref[1]
+    half = buffers[0].shape[0]
+    hidden = hid_refs[0].shape[2]
+    copies = []
+    for k in range(dp):
+        there = pl.ds(pl.multiple_of(lax.rem(replica + dp - k, dp) * hidden, 128), hidden)
+        here = pl.ds(k * hidden, hidden)
+        for step in range(half // tile):
+            rows = pl.ds(step * tile, tile)
+            columns = pl.ds(pl.multiple_of(replica * half + step * tile, 128), tile)
+            for which, left in enumerate((norm_ref, up_ref)):
+                buffer = buffers[which]
+                buffer[rows, here] = contract_first(left[:, columns], hid_refs[k][which]).astype(BF16)
+                copy = pltpu.make_async_copy(
+                    buffer.at[rows, here], targets[which].at[rows, there], sems.at[len(copies)]
+                )
+                copy.start()
+                copies.append(copy)
+    for copy in copies:
+        copy.wait()
 
 
 def finish_kernel(sections, mp, where_ref, recv_ref, rows_ref, saved_ref, gain_ref, act_ref, grad_ref):
@@ -165,45 +228,54 @@
     tokens = dp * block
     vmem = pl.BlockSpec(memory_space=pltpu.VMEM)
     smem = pl.BlockSpec(memory_space=pltpu.SMEM)
-    hbm = pl.BlockSpec(memory_space=pl.ANY)
-
-    to_next = jnp.where(section == sections - 1, new_batch, act_sent[0])
-    to_last = jnp.where(section == 0, loss_grad, grad_sent[0])
-    step = ((jnp.arange(sections) - section) % sections)[:, None, None, None]
-    sent = jnp.where(step == 0, saved_input[0], jnp.where(step == 1, to_next, to_last))
-    sent = jnp.broadcast_to(sent, (sections, mp, mine, width)).reshape(sections * mp, mine, width)
+    hbm = pl.BlockSpec(memory_space=pltpu.HBM)
+
+    params = lambda mib: pltpu.CompilerParams(vmem_limit_bytes=mib * MIB)
+    stay = lambda *arrays: [pltpu.with_memory_space_constraint(x, pltpu.HBM) for x in arrays]
+    like = jax.ShapeDtypeStruct
+    sent = pl.pallas_call(
+        functools.partial(send_kernel, sections, mp),
+        in_specs=[smem] + [hbm] * 5,
+        out_specs=vmem,
+        out_shape=like((sections * mp, mine, width), BF16),
+        scratch_shapes=[pltpu.SemaphoreType.DMA((3,))],
+        compiler_params=params(4),
+        name="send",
+    )(where, *stay(act_sent, new_batch, saved_input, grad_sent, loss_grad))
     got = lax.all_to_all(sent, ("section", "mp"), 0, 0)
     own = got.reshape(sections, block, width)
     rows = [own] + [
         lax.ppermute(own, "dp", [(i, (i + k) % dp) for i in range(dp)]) for k in range(1, dp)
     ]
 
-    chunks = divisor(hidden // 128, 4)
+    chunks = divisor(hidden // 128, 8)
     hid, part, n_bwd, upstream = pl.pallas_call(
-        functools.partial(block_kernel, sections, dp, chunks),
-        in_specs=[smem] + [vmem] * dp + [vmem, hbm, hbm],
+        functools.partial(block_kernel, sections, dp, chunks, 3),
+        in_specs=[smem] + [vmem] * dp + [hbm] * 3,
         out_specs=[vmem] * 4,
         out_shape=[
-            jax.ShapeDtypeStruct((2, tokens, hidden), BF16),
-            jax.ShapeDtypeStruct((dp * mp, 2 * mine, width), BF16),
-            jax.ShapeDtypeStruct((tokens, width), BF16),
-            jax.ShapeDtypeStruct((tokens, width), BF16),
+            like((2, tokens, hidden), BF16),
+            like((dp * mp, 2 * mine, width), BF16),
+            like((tokens, width), BF16),
+            like((tokens, width), BF16),
         ],
         scratch_shapes=[
             pltpu.VMEM((2 * tokens, width), BF16),
+            pltpu.VMEM((1, width), F32),
             pltpu.VMEM((width, hidden), BF16),
             pltpu.VMEM((width, hidden), BF16),
             pltpu.VMEM((tokens, width), F32),
             pltpu.VMEM((tokens, width), F32),
+            pltpu.SemaphoreType.DMA,
             pltpu.SemaphoreType.DMA((chunks,)),
             pltpu.SemaphoreType.DMA((chunks,)),
         ],
-        compiler_params=pltpu.CompilerParams(vmem_limit_bytes=44 * MIB),
+        compiler_params=params(36),
         cost_estimate=pl.CostEstimate(
             flops=12 * tokens * width * hidden, bytes_accessed=4 * width * hidden, transcendentals=2 * tokens * hidden
         ),
         name="block",
-    )(where, *rows, ln_gain, w_in[0], w_out[0])
+    )(where, *rows, *stay(ln_gain, w_in[0], w_out[0]))
 
     hids = [hid] + [
         lax.ppermute(hid, "dp", [(i, (i + k) % dp) for i in range(dp)]) for k in range(1, dp)
@@ -211,41 +283,30 @@
     recv = lax.all_to_all(part, ("dp", "mp"), 0, 0)
 
     half = width // dp
-    tile = 128 * divisor(half // 128, max(1, 6 * 2048 // hidden))
-    steps = half // tile
-    grads = []
-    for k in range(dp):
-        grads = pl.pallas_call(
-            weight_kernel,
-            grid_spec=pltpu.PrefetchScalarGridSpec(
-                num_scalar_prefetch=1,
-                grid=(steps,),
-                in_specs=[
-                    pl.BlockSpec((tokens, tile), lambda i, w: (0, w[1] * steps + i)),
-                    pl.BlockSpec((tokens, tile), lambda i, w: (0, w[1] * steps + i)),
-                    pl.BlockSpec((2, tokens, hidden), lambda i, w: (0, 0, 0)),
-                ]
-                + [hbm] * len(grads),
-                out_specs=[
-                    pl.BlockSpec((tile, hidden), lambda i, w, k=k: (i, lax.rem(w[1] + dp - k, dp)))
-                ]
-                * 2,
-            ),
-            out_shape=[jax.ShapeDtypeStruct((half, dp * hidden), BF16)] * 2,
-            input_output_aliases={4: 0, 5: 1} if grads else {},
-            compiler_params=pltpu.CompilerParams(vmem_limit_bytes=32 * MIB),
-            cost_estimate=pl.CostEstimate(
-                flops=4 * tokens * half * hidden, bytes_accessed=4 * half * hidden, transcendentals=0
-            ),
-            name="weight",
-        )(where, n_bwd, upstream, hids[k], *grads)
+    tile = 128 * divisor(half // 128, 2)
+    grads = pl.pallas_call(
+        functools.partial(weight_kernel, dp, tile),
+        in_specs=[smem] + [vmem] * (2 + dp),
+        out_specs=[hbm] * 2,
+        out_shape=[like((half, dp * hidden), BF16)] * 2,
+        scratch_shapes=[
+            pltpu.VMEM((half, dp * hidden), BF16),
+            pltpu.VMEM((half, dp * hidden), BF16),
+            pltpu.SemaphoreType.DMA((2 * dp * (half // tile),)),
+        ],
+        compiler_params=params(36),
+        cost_estimate=pl.CostEstimate(
+            flops=4 * tokens * half * hidden * dp, bytes_accessed=4 * half * hidden * dp, transcendentals=0
+        ),
+        name="weight",
+    )(where, n_bwd, upstream, *hids)
 
     act_out, grad_out = pl.pallas_call(
         functools.partial(finish_kernel, sections, mp),
         in_specs=[smem] + [vmem] * 4,
         out_specs=[vmem] * 2,
-        out_shape=[jax.ShapeDtypeStruct((1, mine, width), BF16)] * 2,
-        compiler_params=pltpu.CompilerParams(vmem_limit_bytes=16 * MIB),
+        out_shape=[like((1, mine, width), BF16)] * 2,
+        compiler_params=params(16),
         name="finish",
     )(where, recv, got, saved_input, ln_gain)
     return act_out, grad_out, grads[0][None], grads[1][None]

time: 55.7 us -> 52.9 us (0.950)
  other arithmetic: 1.7 us -> 0.08 us
  Pallas kernels: 29.3 us -> 27.9 us
  waiting for transfers between devices: 1.35 us -> 2.6 us
  local copies, waits for them, and re-layouts: 0.89 us -> 0.08 us
    select_n x2 -> x0, other arithmetic: 1.61 us -> none  [the longest x1 0.83 us: per_device(): jnp.where(step == 0, saved_input[0], jnp.where(step == 1, to_next, to_last))]
    pallas_call x3, Pallas kernels: 27.8 us -> 26.3 us  [the longest x1 15.4 us: per_device(): pl.pallas_call(functools.partial(block_kernel, sections, dp, chunks, 3),...]
    ppermute x1, waiting for transfers between devices: 0.01 us -> 1.17 us  [per_device(): lax.ppermute(hid, 'dp', [(i, (i + k) % dp) for i in range(dp)])]
    unnamed x6 -> x4, local copies, waits for them, and re-layouts: 0.71 us -> 0.01 us
  transfers between devices with their start and end apart: 3 -> 3, of which waited for: 1 -> 2; matrix products, arithmetic and copies ran while one was open for 0% -> 0% of each run, Pallas kernels for 23% -> 18%
where the time goes in v2:
time: 52.9 us; the launch traced here: 52.6 us
  Pallas kernels  27.9 us (53%)
  blocking collectives  17.4 us (33%)
  starting transfers between devices  3.9 us (7%)
  waiting for transfers between devices  2.6 us (5%)
  between operations  0.71 us (1%)
    all_to_all x1, blocking collectives, per_device(): got = lax.all_to_all(sent, ('section', 'mp'), 0, 0)  17.4 us
    pallas_call x1, Pallas kernels, per_device(): pl.pallas_call(functools.partial(block_kernel, sections, dp, chunks, 3),...  15.4 us
    pallas_call x1, Pallas kernels, per_device(): pl.pallas_call(functools.partial(weight_kernel, dp, tile), in_specs=[smem...  9.55 us
    all_to_all x1, starting transfers between devices, per_device(): recv = lax.all_to_all(part, ('dp', 'mp'), 0, 0)  3.58 us
    pallas_call x1, Pallas kernels, per_device(): pl.pallas_call(functools.partial(finish_kernel, sections, mp), in_specs=[...  1.51 us
    pallas_call x1, Pallas kernels, per_device(): pl.pallas_call(functools.partial(send_kernel, sections, mp), in_specs=[sm...  1.44 us
    ppermute x1, waiting for transfers between devices, per_device(): lax.ppermute(own, 'dp', [(i, (i + k) % dp) for i in range(dp)])  1.43 us
    ppermute x1, waiting for transfers between devices, per_device(): lax.ppermute(hid, 'dp', [(i, (i + k) % dp) for i in range(dp)])  1.17 us
  transfers between devices with their start and end apart: 3, of which 2 were waited for; matrix products, arithmetic and copies ran while one was open for 0% of the time, Pallas kernels for 18%

profile of v2, /device:TPU:0, one launch (start us, length us, event | category | flops | bytes accessed | tf_op | source)
XLA Modules:
  0.0 52.6 jit_solution(4346305862469542818)
XLA Ops:
  0.6 0.1 pad_add_fusion.where_ref
  0.7 1.4 %send.1 = bf16[16,2,3072]{2,1,0:T(2,128)(2,1)S(1)} custom-call(s32[3]{0:T(128)S(1)} %pad_add_fusion.where_ref, bf16[1,2,3072]{2,1,0:T(2,128)(2,1)} %act_ref.1, bf16[2,3072]{1,0:T(2,128)(2,1)} %batch_ref.1, bf16[1,2,3072]{2,1,0:T(2,128)(2,1)} %saved_ref.3, bf16[1,2,3072]{2,1,0:T(2,128)(2,1)} %grad_ref.1, bf16[2,3072]{1,0:T(2,128)(2,1)} %loss_ref.1), custom_call_target="tpu_custom_call" | custom-call | tf_op jit(solution)/shard_map/send/pallas_call | solution.py:236
  2.2 17.4 %all_to_all.10.rows_ref = bf16[16,2,3072]{2,1,0:T(2,128)(2,1)S(1)} all-to-all(bf16[16,2,3072]{2,1,0:T(2,128)(2,1)S(1)} %send.1), channel_id=1, replica_groups=mesh['section'=4,'dp'=2,'mp'=4] {'section','mp'}, dimensions={0} | all-to-all | bytes 393216 | tf_op jit(solution)/shard_map/all_to_all | solution.py:245
  19.6 0.1 reshape.11.refs_0_
  19.6 0.1 collective-permute-start
  19.7 1.4 %collective-permute-done.refs_1_ = bf16[4,8,3072]{2,1,0:T(8,128)(2,1)S(1)} collective-permute-done((bf16[4,8,3072]{2,1,0:T(8,128)(2,1)S(1)}, bf16[4,8,3072]{2,1,0:T(8,128)(2,1)S(1)}, u32[]{:S(2)}, u32[]{:S(2)}) %collective-permute-start) | collective-permute-done | bytes 196640 | tf_op jit(solution)/shard_map/ppermute | solution.py:248
  21.1 0.0 copy-start
  21.1 0.0 copy-start.1
  21.1 15.4 %block.1 = (bf16[2,16,2048]{2,1,0:T(8,128)(2,1)S(1)}, bf16[8,4,3072]{2,1,0:T(4,128)(2,1)}, bf16[16,3072]{1,0:T(8,128)(2,1)S(1)}, bf16[16,3072]{1,0:T(8,128)(2,1)S(1)}) custom-call(s32[3]{0:T(128)S(1)} %pad_add_fusion.where_ref, bf16[4,8,3072]{2,1,0:T(8,128)(2,1)S(1)} %reshape.11.refs_0_, bf16[4,8,3072]{2,1,0:T(8,128)(2,1)S(1)} %collective-permute-done.refs_1_, ...), custom_call_target="tpu_custom_call" | custom-call | flops 1207959552 | bytes 25165824 | tf_op jit(solution)/shard_map/block/pallas_call | solution.py:252
  36.5 3.6 %all-to-all-start.1 = ((bf16[8,4,3072]{2,1,0:T(4,128)(2,1)}), bf16[8,4,3072]{2,1,0:T(4,128)(2,1)S(1)}, u32[]{:S(2)}, u32[]{:S(2)}) async-start(bf16[8,4,3072]{2,1,0:T(4,128)(2,1)} %get-tuple-element.12), calls=%async_computation.1 | async-start | bytes 393216 | tf_op jit(solution)/shard_map/all_to_all | solution.py:283
  40.1 0.2 collective-permute-start.1
  40.3 1.2 %collective-permute-done.1.refs_1_ = bf16[2,16,2048]{2,1,0:T(8,128)(2,1)S(1)} collective-permute-done((bf16[2,16,2048]{2,1,0:T(8,128)(2,1)S(1)}, bf16[2,16,2048]{2,1,0:T(8,128)(2,1)S(1)}, u32[]{:S(2)}, u32[]{:S(2)}) %collective-permute-start.1) | collective-permute-done | bytes 131104 | tf_op jit(solution)/shard_map/ppermute | solution.py:281
  41.5 9.6 %weight.1 = (bf16[1536,4096]{1,0:T(8,128)(2,1)}, bf16[1536,4096]{1,0:T(8,128)(2,1)}) custom-call(s32[3]{0:T(128)S(1)} %pad_add_fusion.where_ref, bf16[16,3072]{1,0:T(8,128)(2,1)S(1)} %get-tuple-element.15.norm_ref, bf16[16,3072]{1,0:T(8,128)(2,1)S(1)} %get-tuple-element.16.up_ref, bf16[2,16,2048]{2,1,0:T(8,128)(2,1)S(1)} %get-tuple-element.17.refs_0_, ...), custom_call_target="tpu_custom_call" | custom-call | flops 402653184 | bytes 25165824 | tf_op jit(solution)/shard_map/weight/pallas_call | solution.py:287
  51.1 0.0 all-to-all-done.1.recv_ref
  51.1 0.0 copy-done
  51.1 0.0 copy-done.1
  51.1 1.5 %finish.1 = (bf16[1,2,3072]{2,1,0:T(2,128)(2,1)}, bf16[1,2,3072]{2,1,0:T(2,128)(2,1)}) custom-call(s32[3]{0:T(128)S(1)} %pad_add_fusion.where_ref, bf16[8,4,3072]{2,1,0:T(4,128)(2,1)S(1)} %all-to-all-done.1.recv_ref, bf16[16,2,3072]{2,1,0:T(2,128)(2,1)S(1)} %all_to_all.10.rows_ref, bf16[1,2,3072]{2,1,0:T(2,128)(2,1)S(1)} %copy-done.1, f32[1,3072]{1,0:T(1,128)S(1)} %copy-done), custom_call_target="tpu_custom_call" | custom-call | tf_op jit(solution)/shard_map/finish/pallas_call | solution.py:304
Async XLA Ops:
  19.6 1.5 %collective-permute-start = (bf16[4,8,3072]{2,1,0:T(8,128)(2,1)S(1)}, bf16[4,8,3072]{2,1,0:T(8,128)(2,1)S(1)}, u32[]{:S(2)}, u32[]{:S(2)}) collective-permute-start(bf16[4,8,3072]{2,1,0:T(8,128)(2,1)S(1)} %reshape.11.refs_0_), channel_id=1, source_target_pairs={{0,4},{4,0},{1,5},{5,1},{2,6},{6,2},{3,7},{7,3},{8,12},{12,8},{9,1... | collective-permute-start | bytes 589832 | tf_op jit(solution)/shard_map/ppermute | solution.py:248
  21.1 29.9 %copy-start = (f32[1,3072]{1,0:T(1,128)S(1)}, f32[1,3072]{1,0:T(1,128)}, u32[]{:S(2)}) copy-start(f32[1,3072]{1,0:T(1,128)} %gain_ref.1) | copy-start | bytes 36868
  21.1 30.0 %copy-start.1 = (bf16[1,2,3072]{2,1,0:T(2,128)(2,1)S(1)}, bf16[1,2,3072]{2,1,0:T(2,128)(2,1)}, u32[]{:S(2)}) copy-start(bf16[1,2,3072]{2,1,0:T(2,128)(2,1)} %saved_ref.3) | copy-start | bytes 36868
  36.5 14.6 %all-to-all-start.1 = ((bf16[8,4,3072]{2,1,0:T(4,128)(2,1)}), bf16[8,4,3072]{2,1,0:T(4,128)(2,1)S(1)}, u32[]{:S(2)}, u32[]{:S(2)}) async-start(bf16[8,4,3072]{2,1,0:T(4,128)(2,1)} %get-tuple-element.12), calls=%async_computation.1 | async-start | bytes 393216 | tf_op jit(solution)/shard_map/all_to_all | solution.py:283
  40.1 1.4 %collective-permute-start.1 = (bf16[2,16,2048]{2,1,0:T(8,128)(2,1)S(1)}, bf16[2,16,2048]{2,1,0:T(8,128)(2,1)S(1)}, u32[]{:S(2)}, u32[]{:S(2)}) collective-permute-start(bf16[2,16,2048]{2,1,0:T(8,128)(2,1)S(1)} %get-tuple-element.17.refs_0_), channel_id=1, source_target_pairs={{0,4},{4,0},{1,5},{5,1},{2,6},{6,2},{3,7},{7,3},{8,12},{12,8},{9,1... | collective-permute-start | bytes 393224 | tf_op jit(solution)/shard_map/ppermute | solution.py:281

commit v3 on v2

--- a/solution.py
+++ b/solution.py
@@ -46,8 +46,10 @@
     )
 
 
-def send_kernel(sections, mp, where_ref, act_ref, batch_ref, saved_ref, grad_ref, loss_ref, sent_ref, sems):
+def send_kernel(sections, dp, mp, where_ref, act_ref, batch_ref, saved_ref, grad_ref, loss_ref, gain_hbm, win_hbm, wout_hbm, sent_ref, gain_ref, win_ref, wout_ref, sems, near):
     section = where_ref[0]
+    width = win_ref.shape[1]
+    columns = pl.ds(pl.multiple_of(where_ref[1] * (win_hbm.shape[1] // dp), 128), width)
     behind = lax.rem(section + sections - 1, sections)
     ahead = lax.rem(section + 1, sections)
 
@@ -76,49 +78,63 @@
     def _():
         spread(grad_ref.at[0], behind, 2)
 
+    early = [
+        pltpu.make_async_copy(gain_hbm, gain_ref, near.at[0]),
+        pltpu.make_async_copy(win_hbm.at[:, columns], win_ref, near.at[1]),
+        pltpu.make_async_copy(wout_hbm.at[:, columns], wout_ref, near.at[2]),
+    ]
+    for copy in early:
+        copy.start()
     for sem in range(3):
         whole = sent_ref.at[pl.ds(0, mp)]
         pltpu.make_async_copy(whole, whole, sems.at[sem]).wait()
+    for copy in early:
+        copy.wait()
 
 
 def block_kernel(sections, dp, chunks, depth, where_ref, *refs):
     rows_refs = refs[:dp]
-    gain_hbm, win_hbm, wout_hbm = refs[dp : dp + 3]
-    hid_ref, part_ref, norm_ref, up_ref = refs[dp + 3 : dp + 7]
-    both, gain_ref, win, wout, branch, dnorm, sem_gain, sem_in, sem_out = refs[dp + 7 :]
+    gain_ref, win_first, wout_first, win_hbm, wout_hbm = refs[dp : dp + 5]
+    hid_ref, part_ref, norm_ref, up_ref = refs[dp + 5 : dp + 9]
+    both, win, wout, branch, dnorm, sem_in, sem_out = refs[dp + 9 :]
     section, replica = where_ref[0], where_ref[1]
-    block = rows_refs[0].shape[1]
+    lanes = rows_refs[0].shape[0] // sections
+    block = lanes * rows_refs[0].shape[1]
     tokens = dp * block
-    hidden = win.shape[1]
-    width = hidden // chunks
+    width = win_first.shape[1]
+    hidden = chunks * width
     start = replica * hidden
 
     def fetch(chunk):
         source = pl.ds(pl.multiple_of(start + chunk * width, 128), width)
-        target = pl.ds(chunk * width, width)
+        target = pl.ds((chunk - 1) * width, width)
         return (
-            pltpu.make_async_copy(win_hbm.at[:, source], win.at[:, target], sem_in.at[chunk]),
-            pltpu.make_async_copy(wout_hbm.at[:, source], wout.at[:, target], sem_out.at[chunk]),
+            pltpu.make_async_copy(win_hbm.at[:, source], win.at[:, target], sem_in.at[chunk - 1]),
+            pltpu.make_async_copy(wout_hbm.at[:, source], wout.at[:, target], sem_out.at[chunk - 1]),
         )
 
-    fetch_gain = pltpu.make_async_copy(gain_hbm, gain_ref, sem_gain)
-    fetch_gain.start()
-    for chunk in range(min(depth, chunks)):
+    for chunk in range(1, min(depth + 1, chunks)):
         for copy in fetch(chunk):
             copy.start()
 
     behind = lax.rem(section + sections - 1, sections)
     ahead = lax.rem(section + 1, sections)
-    fetch_gain.wait()
     gain = gain_ref[...]
 
     def rows_of(slot, owner):
-        rows = rows_refs[0][slot]
+        here = pl.ds(slot * lanes, lanes)
+        rows = rows_refs[0][here]
         for k in range(1, dp):
             rows = jnp.where(
-                lax.rem(replica + dp - k, dp) == owner, rows_refs[k][slot], rows
+                lax.rem(replica + dp - k, dp) == owner, rows_refs[k][here], rows
             )
-        return rows
+        return rows.reshape(block, rows.shape[-1])
+
+    def weights(chunk):
+        if chunk == 0:
+            return win_first[...], wout_first[...]
+        columns = slice((chunk - 1) * width, chunk * width)
+        return win[:, columns], wout[:, columns]
 
     for owner in range(dp):
         low = owner * block
@@ -132,13 +148,15 @@
 
     def first(chunk):
         columns = slice(chunk * width, (chunk + 1) * width)
-        for copy in fetch(chunk):
-            copy.wait()
-        if chunk + depth < chunks:
-            for copy in fetch(chunk + depth):
-                copy.start()
-        h = jnp.dot(both[...], win[:, columns], preferred_element_type=F32)
-        grad_act = jnp.dot(up_ref[...], wout[:, columns], preferred_element_type=F32)
+        if chunk > 0:
+            for copy in fetch(chunk):
+                copy.wait()
+            if chunk + depth < chunks:
+                for copy in fetch(chunk + depth):
+                    copy.start()
+        w_in, w_out = weights(chunk)
+        h = jnp.dot(both[...], w_in, preferred_element_type=F32)
+        grad_act = jnp.dot(up_ref[...], w_out, preferred_element_type=F32)
         g_fwd = gelu_value(h[:tokens]).astype(BF16)
         g_bwd, slope = gelu_pair(h[tokens:])
         dh = (grad_act * slope).astype(BF16)
@@ -147,9 +165,9 @@
         return g_fwd, dh
 
     def second(chunk, g_fwd, dh):
-        columns = slice(chunk * width, (chunk + 1) * width)
-        term_n = contract_last(dh, win[:, columns])
-        term_b = contract_last(g_fwd, wout[:, columns])
+        w_in, w_out = weights(chunk)
+        term_n = contract_last(dh, w_in)
+        term_b = contract_last(g_fwd, w_out)
         if chunk == 0:
             dnorm[...] = term_n
             branch[...] = term_b
@@ -233,25 +251,31 @@
     params = lambda mib: pltpu.CompilerParams(vmem_limit_bytes=mib * MIB)
     stay = lambda *arrays: [pltpu.with_memory_space_constraint(x, pltpu.HBM) for x in arrays]
     like = jax.ShapeDtypeStruct
-    sent = pl.pallas_call(
-        functools.partial(send_kernel, sections, mp),
-        in_specs=[smem] + [hbm] * 5,
-        out_specs=vmem,
-        out_shape=like((sections * mp, mine, width), BF16),
-        scratch_shapes=[pltpu.SemaphoreType.DMA((3,))],
+    chunks = divisor(hidden // 128, 8)
+    first = hidden // chunks
+    sent, gain, win, wout = pl.pallas_call(
+        functools.partial(send_kernel, sections, dp, mp),
+        in_specs=[smem] + [hbm] * 8,
+        out_specs=[vmem] * 4,
+        out_shape=[
+            like((sections * mp, mine, width), BF16),
+            like((1, width), F32),
+            like((width, first), BF16),
+            like((width, first), BF16),
+        ],
+        scratch_shapes=[pltpu.SemaphoreType.DMA((3,)), pltpu.SemaphoreType.DMA((3,))],
         compiler_params=params(4),
         name="send",
-    )(where, *stay(act_sent, new_batch, saved_input, grad_sent, loss_grad))
+    )(where, *stay(act_sent, new_batch, saved_input, grad_sent, loss_grad, ln_gain, w_in[0], w_out[0]))
     got = lax.all_to_all(sent, ("section", "mp"), 0, 0)
-    own = got.reshape(sections, block, width)
-    rows = [own] + [
-        lax.ppermute(own, "dp", [(i, (i + k) % dp) for i in range(dp)]) for k in range(1, dp)
+    rows = [got] + [
+        lax.ppermute(got, "dp", [(i, (i + k) % dp) for i in range(dp)]) for k in range(1, dp)
     ]
 
-    chunks = divisor(hidden // 128, 8)
+    rest = max(hidden - first, 128)
     hid, part, n_bwd, upstream = pl.pallas_call(
         functools.partial(block_kernel, sections, dp, chunks, 3),
-        in_specs=[smem] + [vmem] * dp + [hbm] * 3,
+        in_specs=[smem] + [vmem] * (dp + 3) + [hbm] * 2,
         out_specs=[vmem] * 4,
         out_shape=[
             like((2, tokens, hidden), BF16),
@@ -261,12 +285,10 @@
         ],
         scratch_shapes=[
             pltpu.VMEM((2 * tokens, width), BF16),
-            pltpu.VMEM((1, width), F32),
-            pltpu.VMEM((width, hidden), BF16),
-            pltpu.VMEM((width, hidden), BF16),
+            pltpu.VMEM((width, rest), BF16),
+            pltpu.VMEM((width, rest), BF16),
             pltpu.VMEM((tokens, width), F32),
             pltpu.VMEM((tokens, width), F32),
-            pltpu.SemaphoreType.DMA,
             pltpu.SemaphoreType.DMA((chunks,)),
             pltpu.SemaphoreType.DMA((chunks,)),
         ],
@@ -275,7 +297,7 @@
             flops=12 * tokens * width * hidden, bytes_accessed=4 * width * hidden, transcendentals=2 * tokens * hidden
         ),
         name="block",
-    )(where, *rows, *stay(ln_gain, w_in[0], w_out[0]))
+    )(where, *rows, gain, win, wout, *stay(w_in[0], w_out[0]))
 
     hids = [hid] + [
         lax.ppermute(hid, "dp", [(i, (i + k) % dp) for i in range(dp)]) for k in range(1, dp)
@@ -308,7 +330,7 @@
         out_shape=[like((1, mine, width), BF16)] * 2,
         compiler_params=params(16),
         name="finish",
-    )(where, recv, got, saved_input, ln_gain)
+    )(where, recv, got, saved_input, gain)
     return act_out, grad_out, grads[0][None], grads[1][None]
 
 

time: 52.9 us -> 51.4 us (0.972)
  Pallas kernels: 27.9 us -> 26.6 us
    pallas_call x1, Pallas kernels: 15.4 us -> 12.9 us  [per_device(): pl.pallas_call(functools.partial(block_kernel, sections, dp, chunks, 3),...]
    pallas_call x1, Pallas kernels: 1.44 us -> 2.66 us  [per_device(): pl.pallas_call(functools.partial(send_kernel, sections, dp, mp), in_specs...]
  transfers between devices with their start and end apart: 3 -> 3, of which waited for: 2 -> 2; matrix products, arithmetic and copies ran while one was open for 0% -> 0% of each run, Pallas kernels for 18% -> 19%
where the time goes in v3:
time: 51.4 us; the launch traced here: 51.1 us
  Pallas kernels  26.6 us (52%)
  blocking collectives  17.3 us (34%)
  starting transfers between devices  3.83 us (7%)
  waiting for transfers between devices  2.61 us (5%)
  between operations  0.69 us (1%)
    all_to_all x1, blocking collectives, per_device(): got = lax.all_to_all(sent, ('section', 'mp'), 0, 0)  17.3 us
    pallas_call x1, Pallas kernels, per_device(): pl.pallas_call(functools.partial(block_kernel, sections, dp, chunks, 3),...  12.9 us
    pallas_call x1, Pallas kernels, per_device(): pl.pallas_call(functools.partial(weight_kernel, dp, tile), in_specs=[smem...  9.55 us
    all_to_all x1, starting transfers between devices, per_device(): recv = lax.all_to_all(part, ('dp', 'mp'), 0, 0)  3.58 us
    pallas_call x1, Pallas kernels, per_device(): pl.pallas_call(functools.partial(send_kernel, sections, dp, mp), in_specs...  2.66 us
    pallas_call x1, Pallas kernels, per_device(): pl.pallas_call(functools.partial(finish_kernel, sections, mp), in_specs=[...  1.51 us
    ppermute x1, waiting for transfers between devices, per_device(): lax.ppermute(got, 'dp', [(i, (i + k) % dp) for i in range(dp)])  1.44 us
    ppermute x1, waiting for transfers between devices, per_device(): lax.ppermute(hid, 'dp', [(i, (i + k) % dp) for i in range(dp)])  1.17 us
  transfers between devices with their start and end apart: 3, of which 2 were waited for; matrix products, arithmetic and copies ran while one was open for 0% of the time, Pallas kernels for 19%

profile of v3, /device:TPU:0, one launch (start us, length us, event | category | flops | bytes accessed | tf_op | source)
XLA Modules:
  0.0 51.1 jit_solution(14105383332609210787)
XLA Ops:
  0.6 0.1 pad_add_fusion.where_ref
  0.7 2.7 %send.1 = (bf16[16,2,3072]{2,1,0:T(2,128)(2,1)S(1)}, f32[1,3072]{1,0:T(1,128)S(1)}, bf16[3072,256]{1,0:T(8,128)(2,1)S(1)}, bf16[3072,256]{1,0:T(8,128)(2,1)S(1)}) custom-call(s32[3]{0:T(128)S(1)} %pad_add_fusion.where_ref, bf16[1,2,3072]{2,1,0:T(2,128)(2,1)} %act_ref.1, bf16[2,3072]{1,0:T(2,128)(2,1)} %batch_ref.1, bf16[1,2,3072]{2,1,0:T(2,128)(2,1)} %saved_ref.3, ...), custom_call_target="tpu_custom_call" | custom-call | tf_op jit(solution)/shard_map/send/pallas_call | solution.py:256
  3.4 17.3 %all_to_all.10.refs_0_.rows_ref = bf16[16,2,3072]{2,1,0:T(2,128)(2,1)S(1)} all-to-all(bf16[16,2,3072]{2,1,0:T(2,128)(2,1)S(1)} %get-tuple-element.16), channel_id=1, replica_groups=mesh['section'=4,'dp'=2,'mp'=4] {'section','mp'}, dimensions={0} | all-to-all | bytes 393216 | tf_op jit(solution)/shard_map/all_to_all | solution.py:270
  20.7 0.0 collective-permute-start
  20.7 1.4 %collective-permute-done.refs_1_ = bf16[16,2,3072]{2,1,0:T(2,128)(2,1)S(1)} collective-permute-done((bf16[16,2,3072]{2,1,0:T(2,128)(2,1)S(1)}, bf16[16,2,3072]{2,1,0:T(2,128)(2,1)S(1)}, u32[]{:S(2)}, u32[]{:S(2)}) %collective-permute-start) | collective-permute-done | bytes 196640 | tf_op jit(solution)/shard_map/ppermute | solution.py:272
  22.1 0.0 copy-start
  22.1 12.9 %block.1 = (bf16[2,16,2048]{2,1,0:T(8,128)(2,1)S(1)}, bf16[8,4,3072]{2,1,0:T(4,128)(2,1)}, bf16[16,3072]{1,0:T(8,128)(2,1)S(1)}, bf16[16,3072]{1,0:T(8,128)(2,1)S(1)}) custom-call(s32[3]{0:T(128)S(1)} %pad_add_fusion.where_ref, bf16[16,2,3072]{2,1,0:T(2,128)(2,1)S(1)} %all_to_all.10.refs_0_.rows_ref, bf16[16,2,3072]{2,1,0:T(2,128)(2,1)S(1)} %collective-permute-done.refs_1_, ...), custom_call_target="tpu_custom_call" | custom-call | flops 1207959552 | bytes 25165824 | tf_op jit(solution)/shard_map/block/pallas_call | solution.py:276
  35.0 3.6 %all-to-all-start.1 = ((bf16[8,4,3072]{2,1,0:T(4,128)(2,1)}), bf16[8,4,3072]{2,1,0:T(4,128)(2,1)S(1)}, u32[]{:S(2)}, u32[]{:S(2)}) async-start(bf16[8,4,3072]{2,1,0:T(4,128)(2,1)} %get-tuple-element.20), calls=%async_computation.1 | async-start | bytes 393216 | tf_op jit(solution)/shard_map/all_to_all | solution.py:305
  38.6 0.2 collective-permute-start.1
  38.9 1.2 %collective-permute-done.1.refs_1_ = bf16[2,16,2048]{2,1,0:T(8,128)(2,1)S(1)} collective-permute-done((bf16[2,16,2048]{2,1,0:T(8,128)(2,1)S(1)}, bf16[2,16,2048]{2,1,0:T(8,128)(2,1)S(1)}, u32[]{:S(2)}, u32[]{:S(2)}) %collective-permute-start.1) | collective-permute-done | bytes 131104 | tf_op jit(solution)/shard_map/ppermute | solution.py:303
  40.0 9.6 %weight.1 = (bf16[1536,4096]{1,0:T(8,128)(2,1)}, bf16[1536,4096]{1,0:T(8,128)(2,1)}) custom-call(s32[3]{0:T(128)S(1)} %pad_add_fusion.where_ref, bf16[16,3072]{1,0:T(8,128)(2,1)S(1)} %get-tuple-element.23.norm_ref, bf16[16,3072]{1,0:T(8,128)(2,1)S(1)} %get-tuple-element.24.up_ref, bf16[2,16,2048]{2,1,0:T(8,128)(2,1)S(1)} %get-tuple-element.25.refs_0_, ...), custom_call_target="tpu_custom_call" | custom-call | flops 402653184 | bytes 25165824 | tf_op jit(solution)/shard_map/weight/pallas_call | solution.py:309
  49.6 0.0 all-to-all-done.1.recv_ref
  49.6 0.0 copy-done
  49.6 1.5 %finish.1 = (bf16[1,2,3072]{2,1,0:T(2,128)(2,1)}, bf16[1,2,3072]{2,1,0:T(2,128)(2,1)}) custom-call(s32[3]{0:T(128)S(1)} %pad_add_fusion.where_ref, bf16[8,4,3072]{2,1,0:T(4,128)(2,1)S(1)} %all-to-all-done.1.recv_ref, bf16[16,2,3072]{2,1,0:T(2,128)(2,1)S(1)} %all_to_all.10.refs_0_.rows_ref, bf16[1,2,3072]{2,1,0:T(2,128)(2,1)S(1)} %copy-done, ...), custom_call_target="tpu_custom_call" | custom-call | tf_op jit(solution)/shard_map/finish/pallas_call | solution.py:326
Async XLA Ops:
  20.7 1.4 %collective-permute-start = (bf16[16,2,3072]{2,1,0:T(2,128)(2,1)S(1)}, bf16[16,2,3072]{2,1,0:T(2,128)(2,1)S(1)}, u32[]{:S(2)}, u32[]{:S(2)}) collective-permute-start(bf16[16,2,3072]{2,1,0:T(2,128)(2,1)S(1)} %all_to_all.10.refs_0_.rows_ref), channel_id=1, source_target_pairs={{0,4},{4,0},{1,5},{5,1},{2,6},{6,2},{3,7},{7,3},{8,12},{12,8},{9,1... | collective-permute-start | bytes 589832 | tf_op jit(solution)/shard_map/ppermute | solution.py:272
  22.1 27.5 %copy-start = (bf16[1,2,3072]{2,1,0:T(2,128)(2,1)S(1)}, bf16[1,2,3072]{2,1,0:T(2,128)(2,1)}, u32[]{:S(2)}) copy-start(bf16[1,2,3072]{2,1,0:T(2,128)(2,1)} %saved_ref.3) | copy-start | bytes 36868
  35.0 14.6 %all-to-all-start.1 = ((bf16[8,4,3072]{2,1,0:T(4,128)(2,1)}), bf16[8,4,3072]{2,1,0:T(4,128)(2,1)S(1)}, u32[]{:S(2)}, u32[]{:S(2)}) async-start(bf16[8,4,3072]{2,1,0:T(4,128)(2,1)} %get-tuple-element.20), calls=%async_computation.1 | async-start | bytes 393216 | tf_op jit(solution)/shard_map/all_to_all | solution.py:305
  38.6 1.4 %collective-permute-start.1 = (bf16[2,16,2048]{2,1,0:T(8,128)(2,1)S(1)}, bf16[2,16,2048]{2,1,0:T(8,128)(2,1)S(1)}, u32[]{:S(2)}, u32[]{:S(2)}) collective-permute-start(bf16[2,16,2048]{2,1,0:T(8,128)(2,1)S(1)} %get-tuple-element.25.refs_0_), channel_id=1, source_target_pairs={{0,4},{4,0},{1,5},{5,1},{2,6},{6,2},{3,7},{7,3},{8,12},{12,8},{9,1... | collective-permute-start | bytes 393224 | tf_op jit(solution)/shard_map/ppermute | solution.py:303

commit v4 on v3

--- a/solution.py
+++ b/solution.py
@@ -46,10 +46,8 @@
     )
 
 
-def send_kernel(sections, dp, mp, where_ref, act_ref, batch_ref, saved_ref, grad_ref, loss_ref, gain_hbm, win_hbm, wout_hbm, sent_ref, gain_ref, win_ref, wout_ref, sems, near):
+def send_kernel(sections, mp, where_ref, act_ref, batch_ref, saved_ref, grad_ref, loss_ref, sent_ref, sems):
     section = where_ref[0]
-    width = win_ref.shape[1]
-    columns = pl.ds(pl.multiple_of(where_ref[1] * (win_hbm.shape[1] // dp), 128), width)
     behind = lax.rem(section + sections - 1, sections)
     ahead = lax.rem(section + 1, sections)
 
@@ -78,17 +76,22 @@
     def _():
         spread(grad_ref.at[0], behind, 2)
 
-    early = [
-        pltpu.make_async_copy(gain_hbm, gain_ref, near.at[0]),
-        pltpu.make_async_copy(win_hbm.at[:, columns], win_ref, near.at[1]),
-        pltpu.make_async_copy(wout_hbm.at[:, columns], wout_ref, near.at[2]),
-    ]
-    for copy in early:
-        copy.start()
     for sem in range(3):
         whole = sent_ref.at[pl.ds(0, mp)]
         pltpu.make_async_copy(whole, whole, sems.at[sem]).wait()
-    for copy in early:
+
+
+def early_kernel(dp, where_ref, gain_hbm, win_hbm, wout_hbm, gain_ref, win_ref, wout_ref, sems):
+    start = where_ref[1] * (win_hbm.shape[1] // dp)
+    columns = pl.ds(pl.multiple_of(start, 128), win_ref.shape[1])
+    copies = [
+        pltpu.make_async_copy(win_hbm.at[:, columns], win_ref, sems.at[0]),
+        pltpu.make_async_copy(gain_hbm, gain_ref, sems.at[1]),
+        pltpu.make_async_copy(wout_hbm.at[:, columns], wout_ref, sems.at[2]),
+    ]
+    for copy in copies:
+        copy.start()
+    for copy in copies:
         copy.wait()
 
 
@@ -251,26 +254,37 @@
     params = lambda mib: pltpu.CompilerParams(vmem_limit_bytes=mib * MIB)
     stay = lambda *arrays: [pltpu.with_memory_space_constraint(x, pltpu.HBM) for x in arrays]
     like = jax.ShapeDtypeStruct
+    sent = pl.pallas_call(
+        functools.partial(send_kernel, sections, mp),
+        in_specs=[smem] + [hbm] * 5,
+        out_specs=vmem,
+        out_shape=like((sections * mp, mine, width), BF16),
+        scratch_shapes=[pltpu.SemaphoreType.DMA((3,))],
+        compiler_params=params(4),
+        name="send",
+    )(where, *stay(act_sent, new_batch, saved_input, grad_sent, loss_grad))
+    got = lax.all_to_all(sent, ("section", "mp"), 0, 0)
     chunks = divisor(hidden // 128, 8)
     first = hidden // chunks
-    sent, gain, win, wout = pl.pallas_call(
-        functools.partial(send_kernel, sections, dp, mp),
-        in_specs=[smem] + [hbm] * 8,
-        out_specs=[vmem] * 4,
+    rows = [got] + [
+        lax.ppermute(got, "dp", [(i, (i + k) % dp) for i in range(dp)]) for k in range(1, dp)
+    ]
+    gain, win, wout = pl.pallas_call(
+        functools.partial(early_kernel, dp),
+        in_specs=[smem] + [hbm] * 3,
+        out_specs=[vmem] * 3,
         out_shape=[
-            like((sections * mp, mine, width), BF16),
             like((1, width), F32),
             like((width, first), BF16),
             like((width, first), BF16),
         ],
-        scratch_shapes=[pltpu.SemaphoreType.DMA((3,)), pltpu.SemaphoreType.DMA((3,))],
+        scratch_shapes=[pltpu.SemaphoreType.DMA((3,))],
         compiler_params=params(4),
-        name="send",
-    )(where, *stay(act_sent, new_batch, saved_input, grad_sent, loss_grad, ln_gain, w_in[0], w_out[0]))
-    got = lax.all_to_all(sent, ("section", "mp"), 0, 0)
-    rows = [got] + [
-        lax.ppermute(got, "dp", [(i, (i + k) % dp) for i in range(dp)]) for k in range(1, dp)
-    ]
+        cost_estimate=pl.CostEstimate(
+            flops=0, bytes_accessed=4 * width * first, transcendentals=0
+        ),
+        name="early",
+    )(where, *stay(ln_gain, w_in[0], w_out[0]))
 
     rest = max(hidden - first, 128)
     hid, part, n_bwd, upstream = pl.pallas_call(

time: 51.4 us -> 51.5 us (level)
  waiting for transfers between devices: 2.61 us -> 1.02 us
  Pallas kernels: 26.6 us -> 27.9 us
    ppermute x1, waiting for transfers between devices: 1.44 us -> 0.01 us  [per_device(): lax.ppermute(got, 'dp', [(i, (i + k) % dp) for i in range(dp)])]
    pallas_call x1 -> x2, Pallas kernels: 2.66 us -> 3.93 us  [the longest x1 2.48 us: per_device(): pl.pallas_call(functools.partial(early_kernel, dp), in_specs=[smem] + [hb...]
  transfers between devices with their start and end apart: 3 -> 3, of which waited for: 2 -> 1; matrix products, arithmetic and copies ran while one was open for 0% -> 0% of each run, Pallas kernels for 19% -> 24%
where the time goes in v4:
time: 51.5 us; the launch traced here: 51.2 us
  Pallas kernels  27.9 us (54%)
  blocking collectives  17.4 us (34%)
  starting transfers between devices  4.11 us (8%)
  waiting for transfers between devices  1.02 us (2%)
  between operations  0.71 us (1%)
    all_to_all x1, blocking collectives, per_device(): got = lax.all_to_all(sent, ('section', 'mp'), 0, 0)  17.4 us
    pallas_call x1, Pallas kernels, per_device(): pl.pallas_call(functools.partial(block_kernel, sections, dp, chunks, 3),...  12.9 us
    pallas_call x1, Pallas kernels, per_device(): pl.pallas_call(functools.partial(weight_kernel, dp, tile), in_specs=[smem...  9.55 us
    all_to_all x1, starting transfers between devices, per_device(): recv = lax.all_to_all(part, ('dp', 'mp'), 0, 0)  3.58 us
    pallas_call x1, Pallas kernels, per_device(): pl.pallas_call(functools.partial(early_kernel, dp), in_specs=[smem] + [hb...  2.48 us
    pallas_call x1, Pallas kernels, per_device(): pl.pallas_call(functools.partial(finish_kernel, sections, mp), in_specs=[...  1.51 us
    pallas_call x1, Pallas kernels, per_device(): pl.pallas_call(functools.partial(send_kernel, sections, mp), in_specs=[sm...  1.44 us
  transfers between devices with their start and end apart: 3, of which 1 were waited for; matrix products, arithmetic and copies ran while one was open for 0% of the time, Pallas kernels for 24%

profile of v4, /device:TPU:0, one launch (start us, length us, event | category | flops | bytes accessed | tf_op | source)
XLA Modules:
  0.0 51.2 jit_solution(14513064834966912764)
XLA Ops:
  0.6 0.1 pad_add_fusion.where_ref
  0.7 1.4 %send.1 = bf16[16,2,3072]{2,1,0:T(2,128)(2,1)S(1)} custom-call(s32[3]{0:T(128)S(1)} %pad_add_fusion.where_ref, bf16[1,2,3072]{2,1,0:T(2,128)(2,1)} %act_ref.1, bf16[2,3072]{1,0:T(2,128)(2,1)} %batch_ref.1, bf16[1,2,3072]{2,1,0:T(2,128)(2,1)} %saved_ref.3, bf16[1,2,3072]{2,1,0:T(2,128)(2,1)} %grad_ref.1, bf16[2,3072]{1,0:T(2,128)(2,1)} %loss_ref.1), custom_call_target="tpu_custom_call" | custom-call | tf_op jit(solution)/shard_map/send/pallas_call | solution.py:257
  2.2 17.4 %all_to_all.10.refs_0_.rows_ref = bf16[16,2,3072]{2,1,0:T(2,128)(2,1)S(1)} all-to-all(bf16[16,2,3072]{2,1,0:T(2,128)(2,1)S(1)} %send.1), channel_id=1, replica_groups=mesh['section'=4,'dp'=2,'mp'=4] {'section','mp'}, dimensions={0} | all-to-all | bytes 393216 | tf_op jit(solution)/shard_map/all_to_all | solution.py:266
  19.6 0.0 collective-permute-start
  19.6 2.5 %early.1 = (f32[1,3072]{1,0:T(1,128)S(1)}, bf16[3072,256]{1,0:T(8,128)(2,1)S(1)}, bf16[3072,256]{1,0:T(8,128)(2,1)S(1)}) custom-call(s32[3]{0:T(128)S(1)} %pad_add_fusion.where_ref, f32[1,3072]{1,0:T(1,128)} %gain_hbm.1, bf16[3072,4096]{1,0:T(8,128)(2,1)} %bitcast.7, bf16[3072,4096]{1,0:T(8,128)(2,1)} %bitcast.9), custom_call_target="tpu_custom_call" | custom-call | bytes 3145728 | tf_op jit(solution)/shard_map/early/pallas_call | solution.py:272
  22.1 0.0 collective-permute-done.refs_1_
  22.1 0.0 copy-start
  22.1 12.9 %block.1 = (bf16[2,16,2048]{2,1,0:T(8,128)(2,1)S(1)}, bf16[8,4,3072]{2,1,0:T(4,128)(2,1)}, bf16[16,3072]{1,0:T(8,128)(2,1)S(1)}, bf16[16,3072]{1,0:T(8,128)(2,1)S(1)}) custom-call(s32[3]{0:T(128)S(1)} %pad_add_fusion.where_ref, bf16[16,2,3072]{2,1,0:T(2,128)(2,1)S(1)} %all_to_all.10.refs_0_.rows_ref, bf16[16,2,3072]{2,1,0:T(2,128)(2,1)S(1)} %collective-permute-done.refs_1_, ...), custom_call_target="tpu_custom_call" | custom-call | flops 1207959552 | bytes 25165824 | tf_op jit(solution)/shard_map/block/pallas_call | solution.py:290
  35.0 3.6 %all-to-all-start.1 = ((bf16[8,4,3072]{2,1,0:T(4,128)(2,1)}), bf16[8,4,3072]{2,1,0:T(4,128)(2,1)S(1)}, u32[]{:S(2)}, u32[]{:S(2)}) async-start(bf16[8,4,3072]{2,1,0:T(4,128)(2,1)} %get-tuple-element.18), calls=%async_computation.1 | async-start | bytes 393216 | tf_op jit(solution)/shard_map/all_to_all | solution.py:319
  38.6 0.5 %collective-permute-start.1 = (bf16[2,16,2048]{2,1,0:T(8,128)(2,1)S(1)}, bf16[2,16,2048]{2,1,0:T(8,128)(2,1)S(1)}, u32[]{:S(2)}, u32[]{:S(2)}) collective-permute-start(bf16[2,16,2048]{2,1,0:T(8,128)(2,1)S(1)} %get-tuple-element.23.refs_0_), channel_id=1, source_target_pairs={{0,4},{4,0},{1,5},{5,1},{2,6},{6,2},{3,7},{7,3},{8,12},{12,8},{9,1... | collective-permute-start | bytes 393224 | tf_op jit(solution)/shard_map/ppermute | solution.py:317
  39.1 1.0 %collective-permute-done.1.refs_1_ = bf16[2,16,2048]{2,1,0:T(8,128)(2,1)S(1)} collective-permute-done((bf16[2,16,2048]{2,1,0:T(8,128)(2,1)S(1)}, bf16[2,16,2048]{2,1,0:T(8,128)(2,1)S(1)}, u32[]{:S(2)}, u32[]{:S(2)}) %collective-permute-start.1) | collective-permute-done | bytes 131104 | tf_op jit(solution)/shard_map/ppermute | solution.py:317
  40.1 9.6 %weight.1 = (bf16[1536,4096]{1,0:T(8,128)(2,1)}, bf16[1536,4096]{1,0:T(8,128)(2,1)}) custom-call(s32[3]{0:T(128)S(1)} %pad_add_fusion.where_ref, bf16[16,3072]{1,0:T(8,128)(2,1)S(1)} %get-tuple-element.21.norm_ref, bf16[16,3072]{1,0:T(8,128)(2,1)S(1)} %get-tuple-element.22.up_ref, bf16[2,16,2048]{2,1,0:T(8,128)(2,1)S(1)} %get-tuple-element.23.refs_0_, ...), custom_call_target="tpu_custom_call" | custom-call | flops 402653184 | bytes 25165824 | tf_op jit(solution)/shard_map/weight/pallas_call | solution.py:323
  49.7 0.0 all-to-all-done.1.recv_ref
  49.7 0.0 copy-done
  49.7 1.5 %finish.1 = (bf16[1,2,3072]{2,1,0:T(2,128)(2,1)}, bf16[1,2,3072]{2,1,0:T(2,128)(2,1)}) custom-call(s32[3]{0:T(128)S(1)} %pad_add_fusion.where_ref, bf16[8,4,3072]{2,1,0:T(4,128)(2,1)S(1)} %all-to-all-done.1.recv_ref, bf16[16,2,3072]{2,1,0:T(2,128)(2,1)S(1)} %all_to_all.10.refs_0_.rows_ref, bf16[1,2,3072]{2,1,0:T(2,128)(2,1)S(1)} %copy-done, ...), custom_call_target="tpu_custom_call" | custom-call | tf_op jit(solution)/shard_map/finish/pallas_call | solution.py:340
Async XLA Ops:
  19.6 2.5 %collective-permute-start = (bf16[16,2,3072]{2,1,0:T(2,128)(2,1)S(1)}, bf16[16,2,3072]{2,1,0:T(2,128)(2,1)S(1)}, u32[]{:S(2)}, u32[]{:S(2)}) collective-permute-start(bf16[16,2,3072]{2,1,0:T(2,128)(2,1)S(1)} %all_to_all.10.refs_0_.rows_ref), channel_id=1, source_target_pairs={{0,4},{4,0},{1,5},{5,1},{2,6},{6,2},{3,7},{7,3},{8,12},{12,8},{9,1... | collective-permute-start | bytes 589832 | tf_op jit(solution)/shard_map/ppermute | solution.py:270
  22.1 27.6 %copy-start = (bf16[1,2,3072]{2,1,0:T(2,128)(2,1)S(1)}, bf16[1,2,3072]{2,1,0:T(2,128)(2,1)}, u32[]{:S(2)}) copy-start(bf16[1,2,3072]{2,1,0:T(2,128)(2,1)} %saved_ref.3) | copy-start | bytes 36868
  35.0 14.7 %all-to-all-start.1 = ((bf16[8,4,3072]{2,1,0:T(4,128)(2,1)}), bf16[8,4,3072]{2,1,0:T(4,128)(2,1)S(1)}, u32[]{:S(2)}, u32[]{:S(2)}) async-start(bf16[8,4,3072]{2,1,0:T(4,128)(2,1)} %get-tuple-element.18), calls=%async_computation.1 | async-start | bytes 393216 | tf_op jit(solution)/shard_map/all_to_all | solution.py:319
  38.6 1.5 %collective-permute-start.1 = (bf16[2,16,2048]{2,1,0:T(8,128)(2,1)S(1)}, bf16[2,16,2048]{2,1,0:T(8,128)(2,1)S(1)}, u32[]{:S(2)}, u32[]{:S(2)}) collective-permute-start(bf16[2,16,2048]{2,1,0:T(8,128)(2,1)S(1)} %get-tuple-element.23.refs_0_), channel_id=1, source_target_pairs={{0,4},{4,0},{1,5},{5,1},{2,6},{6,2},{3,7},{7,3},{8,12},{12,8},{9,1... | collective-permute-start | bytes 393224 | tf_op jit(solution)/shard_map/ppermute | solution.py:317

commit v5 on v3

--- a/solution.py
+++ b/solution.py
@@ -46,10 +46,10 @@
     )
 
 
-def send_kernel(sections, dp, mp, where_ref, act_ref, batch_ref, saved_ref, grad_ref, loss_ref, gain_hbm, win_hbm, wout_hbm, sent_ref, gain_ref, win_ref, wout_ref, sems, near):
-    section = where_ref[0]
+def send_kernel(sections, dp, mp, act_ref, batch_ref, saved_ref, grad_ref, loss_ref, gain_hbm, win_hbm, wout_hbm, sent_ref, gain_ref, win_ref, wout_ref, sems, near):
+    section = lax.axis_index("section")
     width = win_ref.shape[1]
-    columns = pl.ds(pl.multiple_of(where_ref[1] * (win_hbm.shape[1] // dp), 128), width)
+    columns = pl.ds(pl.multiple_of(lax.axis_index("dp") * (win_hbm.shape[1] // dp), 128), width)
     behind = lax.rem(section + sections - 1, sections)
     ahead = lax.rem(section + 1, sections)
 
@@ -92,12 +92,12 @@
         copy.wait()
 
 
-def block_kernel(sections, dp, chunks, depth, where_ref, *refs):
+def block_kernel(sections, dp, chunks, depth, *refs):
     rows_refs = refs[:dp]
     gain_ref, win_first, wout_first, win_hbm, wout_hbm = refs[dp : dp + 5]
     hid_ref, part_ref, norm_ref, up_ref = refs[dp + 5 : dp + 9]
     both, win, wout, branch, dnorm, sem_in, sem_out = refs[dp + 9 :]
-    section, replica = where_ref[0], where_ref[1]
+    section, replica = lax.axis_index("section"), lax.axis_index("dp")
     lanes = rows_refs[0].shape[0] // sections
     block = lanes * rows_refs[0].shape[1]
     tokens = dp * block
@@ -189,10 +189,10 @@
         part_ref[owner, mine:, :] = dnorm[rows, :].astype(BF16)
 
 
-def weight_kernel(dp, tile, where_ref, norm_ref, up_ref, *refs):
+def weight_kernel(dp, tile, norm_ref, up_ref, *refs):
     hid_refs = refs[:dp]
     targets, buffers, sems = refs[dp : dp + 2], refs[dp + 2 : dp + 4], refs[dp + 4]
-    replica = where_ref[1]
+    replica = lax.axis_index("dp")
     half = buffers[0].shape[0]
     hidden = hid_refs[0].shape[2]
     copies = []
@@ -214,8 +214,8 @@
         copy.wait()
 
 
-def finish_kernel(sections, mp, where_ref, recv_ref, rows_ref, saved_ref, gain_ref, act_ref, grad_ref):
-    section, lane = where_ref[0], where_ref[2]
+def finish_kernel(sections, mp, recv_ref, rows_ref, saved_ref, gain_ref, act_ref, grad_ref):
+    section, lane = lax.axis_index("section"), lax.axis_index("mp")
     mine = saved_ref.shape[1]
     total = jnp.sum(recv_ref[...].astype(F32), axis=0)
     behind = lax.rem(section + sections - 1, sections) * mp + lane
@@ -236,16 +236,11 @@
 
 
 def per_device(sections, dp, mp, act_sent, new_batch, saved_input, grad_sent, loss_grad, ln_gain, w_in, w_out):
-    section = lax.axis_index("section")
-    replica = lax.axis_index("dp")
-    lane = lax.axis_index("mp")
-    where = jnp.stack([section, replica, lane]).astype(jnp.int32)
     mine, width = new_batch.shape
     hidden = w_in.shape[2] // dp
     block = mp * mine
     tokens = dp * block
     vmem = pl.BlockSpec(memory_space=pltpu.VMEM)
-    smem = pl.BlockSpec(memory_space=pltpu.SMEM)
     hbm = pl.BlockSpec(memory_space=pltpu.HBM)
 
     params = lambda mib: pltpu.CompilerParams(vmem_limit_bytes=mib * MIB)
@@ -255,7 +250,7 @@
     first = hidden // chunks
     sent, gain, win, wout = pl.pallas_call(
         functools.partial(send_kernel, sections, dp, mp),
-        in_specs=[smem] + [hbm] * 8,
+        in_specs=[hbm] * 8,
         out_specs=[vmem] * 4,
         out_shape=[
             like((sections * mp, mine, width), BF16),
@@ -266,7 +261,7 @@
         scratch_shapes=[pltpu.SemaphoreType.DMA((3,)), pltpu.SemaphoreType.DMA((3,))],
         compiler_params=params(4),
         name="send",
-    )(where, *stay(act_sent, new_batch, saved_input, grad_sent, loss_grad, ln_gain, w_in[0], w_out[0]))
+    )(*stay(act_sent, new_batch, saved_input, grad_sent, loss_grad, ln_gain, w_in[0], w_out[0]))
     got = lax.all_to_all(sent, ("section", "mp"), 0, 0)
     rows = [got] + [
         lax.ppermute(got, "dp", [(i, (i + k) % dp) for i in range(dp)]) for k in range(1, dp)
@@ -275,7 +270,7 @@
     rest = max(hidden - first, 128)
     hid, part, n_bwd, upstream = pl.pallas_call(
         functools.partial(block_kernel, sections, dp, chunks, 3),
-        in_specs=[smem] + [vmem] * (dp + 3) + [hbm] * 2,
+        in_specs=[vmem] * (dp + 3) + [hbm] * 2,
         out_specs=[vmem] * 4,
         out_shape=[
             like((2, tokens, hidden), BF16),
@@ -297,7 +292,7 @@
             flops=12 * tokens * width * hidden, bytes_accessed=4 * width * hidden, transcendentals=2 * tokens * hidden
         ),
         name="block",
-    )(where, *rows, gain, win, wout, *stay(w_in[0], w_out[0]))
+    )(*rows, gain, win, wout, *stay(w_in[0], w_out[0]))
 
     hids = [hid] + [
         lax.ppermute(hid, "dp", [(i, (i + k) % dp) for i in range(dp)]) for k in range(1, dp)
@@ -308,7 +303,7 @@
     tile = 128 * divisor(half // 128, 2)
     grads = pl.pallas_call(
         functools.partial(weight_kernel, dp, tile),
-        in_specs=[smem] + [vmem] * (2 + dp),
+        in_specs=[vmem] * (2 + dp),
         out_specs=[hbm] * 2,
         out_shape=[like((half, dp * hidden), BF16)] * 2,
         scratch_shapes=[
@@ -321,16 +316,16 @@
             flops=4 * tokens * half * hidden * dp, bytes_accessed=4 * half * hidden * dp, transcendentals=0
         ),
         name="weight",
-    )(where, n_bwd, upstream, *hids)
+    )(n_bwd, upstream, *hids)
 
     act_out, grad_out = pl.pallas_call(
         functools.partial(finish_kernel, sections, mp),
-        in_specs=[smem] + [vmem] * 4,
+        in_specs=[vmem] * 4,
         out_specs=[vmem] * 2,
         out_shape=[like((1, mine, width), BF16)] * 2,
         compiler_params=params(16),
         name="finish",
-    )(where, recv, got, saved_input, gain)
+    )(recv, got, saved_input, gain)
     return act_out, grad_out, grads[0][None], grads[1][None]
 
 

time: 51.4 us -> 49.4 us (0.961)
  Pallas kernels: 26.6 us -> 24.7 us
    pallas_call x1, Pallas kernels: 1.51 us -> 0.97 us  [per_device(): pl.pallas_call(functools.partial(finish_kernel, sections, mp), in_specs=[...]
    pallas_call x1, Pallas kernels: 9.55 us -> 9.01 us  [per_device(): pl.pallas_call(functools.partial(weight_kernel, dp, tile), in_specs=[vmem...]
    pallas_call x1, Pallas kernels: 2.66 us -> 2.12 us  [per_device(): pl.pallas_call(functools.partial(send_kernel, sections, dp, mp), in_specs...]
  transfers between devices with their start and end apart: 3 -> 3, of which waited for: 2 -> 2; matrix products, arithmetic and copies ran while one was open for 0% -> 0% of each run, Pallas kernels for 19% -> 18%
where the time goes in v5:
time: 49.4 us; the launch traced here: 49.2 us
  Pallas kernels  24.7 us (50%)
  blocking collectives  17.3 us (35%)
  starting transfers between devices  3.83 us (8%)
  waiting for transfers between devices  2.61 us (5%)
  between operations  0.68 us (1%)
    all_to_all x1, blocking collectives, per_device(): got = lax.all_to_all(sent, ('section', 'mp'), 0, 0)  17.3 us
    pallas_call x1, Pallas kernels, per_device(): pl.pallas_call(functools.partial(block_kernel, sections, dp, chunks, 3),...  12.6 us
    pallas_call x1, Pallas kernels, per_device(): pl.pallas_call(functools.partial(weight_kernel, dp, tile), in_specs=[vmem...  9.01 us
    all_to_all x1, starting transfers between devices, per_device(): recv = lax.all_to_all(part, ('dp', 'mp'), 0, 0)  3.58 us
    pallas_call x1, Pallas kernels, per_device(): pl.pallas_call(functools.partial(send_kernel, sections, dp, mp), in_specs...  2.12 us
    ppermute x1, waiting for transfers between devices, per_device(): lax.ppermute(got, 'dp', [(i, (i + k) % dp) for i in range(dp)])  1.44 us
    ppermute x1, waiting for transfers between devices, per_device(): lax.ppermute(hid, 'dp', [(i, (i + k) % dp) for i in range(dp)])  1.17 us
  transfers between devices with their start and end apart: 3, of which 2 were waited for; matrix products, arithmetic and copies ran while one was open for 0% of the time, Pallas kernels for 18%

profile of v5, /device:TPU:0, one launch (start us, length us, event | category | flops | bytes accessed | tf_op | source)
XLA Modules:
  0.0 49.2 jit_solution(8791580365273434333)
XLA Ops:
  0.6 2.1 %send.1 = (bf16[16,2,3072]{2,1,0:T(2,128)(2,1)S(1)}, f32[1,3072]{1,0:T(1,128)S(1)}, bf16[3072,256]{1,0:T(8,128)(2,1)S(1)}, bf16[3072,256]{1,0:T(8,128)(2,1)S(1)}) custom-call(bf16[1,2,3072]{2,1,0:T(2,128)(2,1)} %act_ref.1, bf16[2,3072]{1,0:T(2,128)(2,1)} %batch_ref.1, bf16[1,2,3072]{2,1,0:T(2,128)(2,1)} %saved_ref.3, bf16[1,2,3072]{2,1,0:T(2,128)(2,1)} %grad_ref.1, ...), custom_call_target="tpu_custom_call" | custom-call | tf_op jit(solution)/shard_map/send/pallas_call | solution.py:251
  2.8 17.3 %all_to_all.10.refs_0_.rows_ref = bf16[16,2,3072]{2,1,0:T(2,128)(2,1)S(1)} all-to-all(bf16[16,2,3072]{2,1,0:T(2,128)(2,1)S(1)} %get-tuple-element.16), channel_id=1, replica_groups=mesh['section'=4,'dp'=2,'mp'=4] {'section','mp'}, dimensions={0} | all-to-all | bytes 393216 | tf_op jit(solution)/shard_map/all_to_all | solution.py:265
  20.1 0.0 collective-permute-start
  20.1 1.4 %collective-permute-done.refs_1_ = bf16[16,2,3072]{2,1,0:T(2,128)(2,1)S(1)} collective-permute-done((bf16[16,2,3072]{2,1,0:T(2,128)(2,1)S(1)}, bf16[16,2,3072]{2,1,0:T(2,128)(2,1)S(1)}, u32[]{:S(2)}, u32[]{:S(2)}) %collective-permute-start) | collective-permute-done | bytes 196640 | tf_op jit(solution)/shard_map/ppermute | solution.py:267
  21.5 0.0 copy-start
  21.5 12.6 %block.1 = (bf16[2,16,2048]{2,1,0:T(8,128)(2,1)S(1)}, bf16[8,4,3072]{2,1,0:T(4,128)(2,1)}, bf16[16,3072]{1,0:T(8,128)(2,1)S(1)}, bf16[16,3072]{1,0:T(8,128)(2,1)S(1)}) custom-call(bf16[16,2,3072]{2,1,0:T(2,128)(2,1)S(1)} %all_to_all.10.refs_0_.rows_ref, bf16[16,2,3072]{2,1,0:T(2,128)(2,1)S(1)} %collective-permute-done.refs_1_, ...), custom_call_target="tpu_custom_call" | custom-call | flops 1207959552 | bytes 25165824 | tf_op jit(solution)/shard_map/block/pallas_call | solution.py:271
  34.2 3.6 %all-to-all-start.1 = ((bf16[8,4,3072]{2,1,0:T(4,128)(2,1)}), bf16[8,4,3072]{2,1,0:T(4,128)(2,1)S(1)}, u32[]{:S(2)}, u32[]{:S(2)}) async-start(bf16[8,4,3072]{2,1,0:T(4,128)(2,1)} %get-tuple-element.20), calls=%async_computation.1 | async-start | bytes 393216 | tf_op jit(solution)/shard_map/all_to_all | solution.py:300
  37.8 0.2 collective-permute-start.1
  38.0 1.2 %collective-permute-done.1.refs_1_ = bf16[2,16,2048]{2,1,0:T(8,128)(2,1)S(1)} collective-permute-done((bf16[2,16,2048]{2,1,0:T(8,128)(2,1)S(1)}, bf16[2,16,2048]{2,1,0:T(8,128)(2,1)S(1)}, u32[]{:S(2)}, u32[]{:S(2)}) %collective-permute-start.1) | collective-permute-done | bytes 131104 | tf_op jit(solution)/shard_map/ppermute | solution.py:298
  39.2 9.0 %weight.1 = (bf16[1536,4096]{1,0:T(8,128)(2,1)}, bf16[1536,4096]{1,0:T(8,128)(2,1)}) custom-call(bf16[16,3072]{1,0:T(8,128)(2,1)S(1)} %get-tuple-element.23.norm_ref, bf16[16,3072]{1,0:T(8,128)(2,1)S(1)} %get-tuple-element.24.up_ref, bf16[2,16,2048]{2,1,0:T(8,128)(2,1)S(1)} %get-tuple-element.25.refs_0_, bf16[2,16,2048]{2,1,0:T(8,128)(2,1)S(1)} %collective-permute-done.1.refs_1_), custom_call_target="tpu_custom_call" | custom-call | flops 402653184 | bytes 25165824 | tf_op jit(solution)/shard_map/weight/pallas_call | solution.py:304
  48.2 0.0 all-to-all-done.1.recv_ref
  48.2 0.0 copy-done
  48.2 1.0 %finish.1 = (bf16[1,2,3072]{2,1,0:T(2,128)(2,1)}, bf16[1,2,3072]{2,1,0:T(2,128)(2,1)}) custom-call(bf16[8,4,3072]{2,1,0:T(4,128)(2,1)S(1)} %all-to-all-done.1.recv_ref, bf16[16,2,3072]{2,1,0:T(2,128)(2,1)S(1)} %all_to_all.10.refs_0_.rows_ref, bf16[1,2,3072]{2,1,0:T(2,128)(2,1)S(1)} %copy-done, f32[1,3072]{1,0:T(1,128)S(1)} %get-tuple-element.17.refs_2_.gain_ref), custom_call_target="tpu_custom_call" | custom-call | tf_op jit(solution)/shard_map/finish/pallas_call | solution.py:321
Async XLA Ops:
  20.1 1.4 %collective-permute-start = (bf16[16,2,3072]{2,1,0:T(2,128)(2,1)S(1)}, bf16[16,2,3072]{2,1,0:T(2,128)(2,1)S(1)}, u32[]{:S(2)}, u32[]{:S(2)}) collective-permute-start(bf16[16,2,3072]{2,1,0:T(2,128)(2,1)S(1)} %all_to_all.10.refs_0_.rows_ref), channel_id=1, source_target_pairs={{0,4},{4,0},{1,5},{5,1},{2,6},{6,2},{3,7},{7,3},{8,12},{12,8},{9,1... | collective-permute-start | bytes 589832 | tf_op jit(solution)/shard_map/ppermute | solution.py:267
  21.5 26.7 %copy-start = (bf16[1,2,3072]{2,1,0:T(2,128)(2,1)S(1)}, bf16[1,2,3072]{2,1,0:T(2,128)(2,1)}, u32[]{:S(2)}) copy-start(bf16[1,2,3072]{2,1,0:T(2,128)(2,1)} %saved_ref.3) | copy-start | bytes 36868
  34.2 14.0 %all-to-all-start.1 = ((bf16[8,4,3072]{2,1,0:T(4,128)(2,1)}), bf16[8,4,3072]{2,1,0:T(4,128)(2,1)S(1)}, u32[]{:S(2)}, u32[]{:S(2)}) async-start(bf16[8,4,3072]{2,1,0:T(4,128)(2,1)} %get-tuple-element.20), calls=%async_computation.1 | async-start | bytes 393216 | tf_op jit(solution)/shard_map/all_to_all | solution.py:300
  37.8 1.4 %collective-permute-start.1 = (bf16[2,16,2048]{2,1,0:T(8,128)(2,1)S(1)}, bf16[2,16,2048]{2,1,0:T(8,128)(2,1)S(1)}, u32[]{:S(2)}, u32[]{:S(2)}) collective-permute-start(bf16[2,16,2048]{2,1,0:T(8,128)(2,1)S(1)} %get-tuple-element.25.refs_0_), channel_id=1, source_target_pairs={{0,4},{4,0},{1,5},{5,1},{2,6},{6,2},{3,7},{7,3},{8,12},{12,8},{9,1... | collective-permute-start | bytes 393224 | tf_op jit(solution)/shard_map/ppermute | solution.py:298

commit v6 on v4

--- a/solution.py
+++ b/solution.py
@@ -46,8 +46,8 @@
     )
 
 
-def send_kernel(sections, mp, where_ref, act_ref, batch_ref, saved_ref, grad_ref, loss_ref, sent_ref, sems):
-    section = where_ref[0]
+def send_kernel(sections, mp, act_ref, batch_ref, saved_ref, grad_ref, loss_ref, sent_ref, sems):
+    section = lax.axis_index("section")
     behind = lax.rem(section + sections - 1, sections)
     ahead = lax.rem(section + 1, sections)
 
@@ -81,8 +81,8 @@
         pltpu.make_async_copy(whole, whole, sems.at[sem]).wait()
 
 
-def early_kernel(dp, where_ref, gain_hbm, win_hbm, wout_hbm, gain_ref, win_ref, wout_ref, sems):
-    start = where_ref[1] * (win_hbm.shape[1] // dp)
+def early_kernel(dp, gain_hbm, win_hbm, wout_hbm, gain_ref, win_ref, wout_ref, sems):
+    start = lax.axis_index("dp") * (win_hbm.shape[1] // dp)
     columns = pl.ds(pl.multiple_of(start, 128), win_ref.shape[1])
     copies = [
         pltpu.make_async_copy(win_hbm.at[:, columns], win_ref, sems.at[0]),
@@ -95,12 +95,12 @@
         copy.wait()
 
 
-def block_kernel(sections, dp, chunks, depth, where_ref, *refs):
+def block_kernel(sections, dp, chunks, depth, *refs):
     rows_refs = refs[:dp]
     gain_ref, win_first, wout_first, win_hbm, wout_hbm = refs[dp : dp + 5]
     hid_ref, part_ref, norm_ref, up_ref = refs[dp + 5 : dp + 9]
     both, win, wout, branch, dnorm, sem_in, sem_out = refs[dp + 9 :]
-    section, replica = where_ref[0], where_ref[1]
+    section, replica = lax.axis_index("section"), lax.axis_index("dp")
     lanes = rows_refs[0].shape[0] // sections
     block = lanes * rows_refs[0].shape[1]
     tokens = dp * block
@@ -192,10 +192,10 @@
         part_ref[owner, mine:, :] = dnorm[rows, :].astype(BF16)
 
 
-def weight_kernel(dp, tile, where_ref, norm_ref, up_ref, *refs):
+def weight_kernel(dp, tile, norm_ref, up_ref, *refs):
     hid_refs = refs[:dp]
     targets, buffers, sems = refs[dp : dp + 2], refs[dp + 2 : dp + 4], refs[dp + 4]
-    replica = where_ref[1]
+    replica = lax.axis_index("dp")
     half = buffers[0].shape[0]
     hidden = hid_refs[0].shape[2]
     copies = []
@@ -217,8 +217,8 @@
         copy.wait()
 
 
-def finish_kernel(sections, mp, where_ref, recv_ref, rows_ref, saved_ref, gain_ref, act_ref, grad_ref):
-    section, lane = where_ref[0], where_ref[2]
+def finish_kernel(sections, mp, recv_ref, rows_ref, saved_ref, gain_ref, act_ref, grad_ref):
+    section, lane = lax.axis_index("section"), lax.axis_index("mp")
     mine = saved_ref.shape[1]
     total = jnp.sum(recv_ref[...].astype(F32), axis=0)
     behind = lax.rem(section + sections - 1, sections) * mp + lane
@@ -239,16 +239,11 @@
 
 
 def per_device(sections, dp, mp, act_sent, new_batch, saved_input, grad_sent, loss_grad, ln_gain, w_in, w_out):
-    section = lax.axis_index("section")
-    replica = lax.axis_index("dp")
-    lane = lax.axis_index("mp")
-    where = jnp.stack([section, replica, lane]).astype(jnp.int32)
     mine, width = new_batch.shape
     hidden = w_in.shape[2] // dp
     block = mp * mine
     tokens = dp * block
     vmem = pl.BlockSpec(memory_space=pltpu.VMEM)
-    smem = pl.BlockSpec(memory_space=pltpu.SMEM)
     hbm = pl.BlockSpec(memory_space=pltpu.HBM)
 
     params = lambda mib: pltpu.CompilerParams(vmem_limit_bytes=mib * MIB)
@@ -256,13 +251,13 @@
     like = jax.ShapeDtypeStruct
     sent = pl.pallas_call(
         functools.partial(send_kernel, sections, mp),
-        in_specs=[smem] + [hbm] * 5,
+        in_specs=[hbm] * 5,
         out_specs=vmem,
         out_shape=like((sections * mp, mine, width), BF16),
         scratch_shapes=[pltpu.SemaphoreType.DMA((3,))],
         compiler_params=params(4),
         name="send",
-    )(where, *stay(act_sent, new_batch, saved_input, grad_sent, loss_grad))
+    )(*stay(act_sent, new_batch, saved_input, grad_sent, loss_grad))
     got = lax.all_to_all(sent, ("section", "mp"), 0, 0)
     chunks = divisor(hidden // 128, 8)
     first = hidden // chunks
@@ -271,7 +266,7 @@
     ]
     gain, win, wout = pl.pallas_call(
         functools.partial(early_kernel, dp),
-        in_specs=[smem] + [hbm] * 3,
+        in_specs=[hbm] * 3,
         out_specs=[vmem] * 3,
         out_shape=[
             like((1, width), F32),
@@ -284,12 +279,12 @@
             flops=0, bytes_accessed=4 * width * first, transcendentals=0
         ),
         name="early",
-    )(where, *stay(ln_gain, w_in[0], w_out[0]))
+    )(*stay(ln_gain, w_in[0], w_out[0]))
 
     rest = max(hidden - first, 128)
     hid, part, n_bwd, upstream = pl.pallas_call(
         functools.partial(block_kernel, sections, dp, chunks, 3),
-        in_specs=[smem] + [vmem] * (dp + 3) + [hbm] * 2,
+        in_specs=[vmem] * (dp + 3) + [hbm] * 2,
         out_specs=[vmem] * 4,
         out_shape=[
             like((2, tokens, hidden), BF16),
@@ -311,7 +306,7 @@
             flops=12 * tokens * width * hidden, bytes_accessed=4 * width * hidden, transcendentals=2 * tokens * hidden
         ),
         name="block",
-    )(where, *rows, gain, win, wout, *stay(w_in[0], w_out[0]))
+    )(*rows, gain, win, wout, *stay(w_in[0], w_out[0]))
 
     hids = [hid] + [
         lax.ppermute(hid, "dp", [(i, (i + k) % dp) for i in range(dp)]) for k in range(1, dp)
@@ -322,7 +317,7 @@
     tile = 128 * divisor(half // 128, 2)
     grads = pl.pallas_call(
         functools.partial(weight_kernel, dp, tile),
-        in_specs=[smem] + [vmem] * (2 + dp),
+        in_specs=[vmem] * (2 + dp),
         out_specs=[hbm] * 2,
         out_shape=[like((half, dp * hidden), BF16)] * 2,
         scratch_shapes=[
@@ -335,16 +330,16 @@
             flops=4 * tokens * half * hidden * dp, bytes_accessed=4 * half * hidden * dp, transcendentals=0
         ),
         name="weight",
-    )(where, n_bwd, upstream, *hids)
+    )(n_bwd, upstream, *hids)
 
     act_out, grad_out = pl.pallas_call(
         functools.partial(finish_kernel, sections, mp),
-        in_specs=[smem] + [vmem] * 4,
+        in_specs=[vmem] * 4,
         out_specs=[vmem] * 2,
         out_shape=[like((1, mine, width), BF16)] * 2,
         compiler_params=params(16),
         name="finish",
-    )(where, recv, got, saved_input, gain)
+    )(recv, got, saved_input, gain)
     return act_out, grad_out, grads[0][None], grads[1][None]
 
 

time: 51.5 us -> 49 us (0.951)
  Pallas kernels: 27.9 us -> 25.5 us
    pallas_call x3, Pallas kernels: 13.5 us -> 11.9 us  [the longest x1 9.01 us: per_device(): pl.pallas_call(functools.partial(weight_kernel, dp, tile), in_specs=[vmem...]
    pallas_call x1, Pallas kernels: 1.51 us -> 0.97 us  [per_device(): pl.pallas_call(functools.partial(finish_kernel, sections, mp), in_specs=[...]
  transfers between devices with their start and end apart: 3 -> 3, of which waited for: 1 -> 1; matrix products, arithmetic and copies ran while one was open for 0% -> 0% of each run, Pallas kernels for 24% -> 22%
where the time goes in v6:
time: 49 us; the launch traced here: 48.7 us
  Pallas kernels  25.5 us (52%)
  blocking collectives  17.4 us (36%)
  starting transfers between devices  4.11 us (8%)
  waiting for transfers between devices  1.02 us (2%)
  between operations  0.71 us (1%)
    all_to_all x1, blocking collectives, per_device(): got = lax.all_to_all(sent, ('section', 'mp'), 0, 0)  17.4 us
    pallas_call x1, Pallas kernels, per_device(): pl.pallas_call(functools.partial(block_kernel, sections, dp, chunks, 3),...  12.6 us
    pallas_call x1, Pallas kernels, per_device(): pl.pallas_call(functools.partial(weight_kernel, dp, tile), in_specs=[vmem...  9.01 us
    all_to_all x1, starting transfers between devices, per_device(): recv = lax.all_to_all(part, ('dp', 'mp'), 0, 0)  3.58 us
    pallas_call x1, Pallas kernels, per_device(): pl.pallas_call(functools.partial(early_kernel, dp), in_specs=[hbm] * 3, o...  1.94 us
    ppermute x1, waiting for transfers between devices, per_device(): lax.ppermute(hid, 'dp', [(i, (i + k) % dp) for i in range(dp)])  1.01 us
  transfers between devices with their start and end apart: 3, of which 1 were waited for; matrix products, arithmetic and copies ran while one was open for 0% of the time, Pallas kernels for 22%

profile of v6, /device:TPU:0, one launch (start us, length us, event | category | flops | bytes accessed | tf_op | source)
XLA Modules:
  0.0 48.7 jit_solution(4089302179500554954)
XLA Ops:
  0.6 0.9 %send.1 = bf16[16,2,3072]{2,1,0:T(2,128)(2,1)S(1)} custom-call(bf16[1,2,3072]{2,1,0:T(2,128)(2,1)} %act_ref.1, bf16[2,3072]{1,0:T(2,128)(2,1)} %batch_ref.1, bf16[1,2,3072]{2,1,0:T(2,128)(2,1)} %saved_ref.3, bf16[1,2,3072]{2,1,0:T(2,128)(2,1)} %grad_ref.1, bf16[2,3072]{1,0:T(2,128)(2,1)} %loss_ref.1), custom_call_target="tpu_custom_call" | custom-call | tf_op jit(solution)/shard_map/send/pallas_call | solution.py:252
  1.5 17.4 %all_to_all.10.refs_0_.rows_ref = bf16[16,2,3072]{2,1,0:T(2,128)(2,1)S(1)} all-to-all(bf16[16,2,3072]{2,1,0:T(2,128)(2,1)S(1)} %send.1), channel_id=1, replica_groups=mesh['section'=4,'dp'=2,'mp'=4] {'section','mp'}, dimensions={0} | all-to-all | bytes 393216 | tf_op jit(solution)/shard_map/all_to_all | solution.py:261
  18.9 0.0 collective-permute-start
  18.9 1.9 %early.1 = (f32[1,3072]{1,0:T(1,128)S(1)}, bf16[3072,256]{1,0:T(8,128)(2,1)S(1)}, bf16[3072,256]{1,0:T(8,128)(2,1)S(1)}) custom-call(f32[1,3072]{1,0:T(1,128)} %gain_hbm.1, bf16[3072,4096]{1,0:T(8,128)(2,1)} %bitcast.4, bf16[3072,4096]{1,0:T(8,128)(2,1)} %bitcast.6), custom_call_target="tpu_custom_call" | custom-call | bytes 3145728 | tf_op jit(solution)/shard_map/early/pallas_call | solution.py:267
  20.9 0.0 collective-permute-done.refs_1_
  20.9 0.0 copy-start
  20.9 12.6 %block.1 = (bf16[2,16,2048]{2,1,0:T(8,128)(2,1)S(1)}, bf16[8,4,3072]{2,1,0:T(4,128)(2,1)}, bf16[16,3072]{1,0:T(8,128)(2,1)S(1)}, bf16[16,3072]{1,0:T(8,128)(2,1)S(1)}) custom-call(bf16[16,2,3072]{2,1,0:T(2,128)(2,1)S(1)} %all_to_all.10.refs_0_.rows_ref, bf16[16,2,3072]{2,1,0:T(2,128)(2,1)S(1)} %collective-permute-done.refs_1_, ...), custom_call_target="tpu_custom_call" | custom-call | flops 1207959552 | bytes 25165824 | tf_op jit(solution)/shard_map/block/pallas_call | solution.py:285
  33.6 3.6 %all-to-all-start.1 = ((bf16[8,4,3072]{2,1,0:T(4,128)(2,1)}), bf16[8,4,3072]{2,1,0:T(4,128)(2,1)S(1)}, u32[]{:S(2)}, u32[]{:S(2)}) async-start(bf16[8,4,3072]{2,1,0:T(4,128)(2,1)} %get-tuple-element.18), calls=%async_computation.1 | async-start | bytes 393216 | tf_op jit(solution)/shard_map/all_to_all | solution.py:314
  37.2 0.5 %collective-permute-start.1 = (bf16[2,16,2048]{2,1,0:T(8,128)(2,1)S(1)}, bf16[2,16,2048]{2,1,0:T(8,128)(2,1)S(1)}, u32[]{:S(2)}, u32[]{:S(2)}) collective-permute-start(bf16[2,16,2048]{2,1,0:T(8,128)(2,1)S(1)} %get-tuple-element.23.refs_0_), channel_id=1, source_target_pairs={{0,4},{4,0},{1,5},{5,1},{2,6},{6,2},{3,7},{7,3},{8,12},{12,8},{9,1... | collective-permute-start | bytes 393224 | tf_op jit(solution)/shard_map/ppermute | solution.py:312
  37.7 1.0 %collective-permute-done.1.refs_1_ = bf16[2,16,2048]{2,1,0:T(8,128)(2,1)S(1)} collective-permute-done((bf16[2,16,2048]{2,1,0:T(8,128)(2,1)S(1)}, bf16[2,16,2048]{2,1,0:T(8,128)(2,1)S(1)}, u32[]{:S(2)}, u32[]{:S(2)}) %collective-permute-start.1) | collective-permute-done | bytes 131104 | tf_op jit(solution)/shard_map/ppermute | solution.py:312
  38.7 9.0 %weight.1 = (bf16[1536,4096]{1,0:T(8,128)(2,1)}, bf16[1536,4096]{1,0:T(8,128)(2,1)}) custom-call(bf16[16,3072]{1,0:T(8,128)(2,1)S(1)} %get-tuple-element.21.norm_ref, bf16[16,3072]{1,0:T(8,128)(2,1)S(1)} %get-tuple-element.22.up_ref, bf16[2,16,2048]{2,1,0:T(8,128)(2,1)S(1)} %get-tuple-element.23.refs_0_, bf16[2,16,2048]{2,1,0:T(8,128)(2,1)S(1)} %collective-permute-done.1.refs_1_), custom_call_target="tpu_custom_call" | custom-call | flops 402653184 | bytes 25165824 | tf_op jit(solution)/shard_map/weight/pallas_call | solution.py:318
  47.7 0.0 all-to-all-done.1.recv_ref
  47.7 0.0 copy-done
  47.7 1.0 %finish.1 = (bf16[1,2,3072]{2,1,0:T(2,128)(2,1)}, bf16[1,2,3072]{2,1,0:T(2,128)(2,1)}) custom-call(bf16[8,4,3072]{2,1,0:T(4,128)(2,1)S(1)} %all-to-all-done.1.recv_ref, bf16[16,2,3072]{2,1,0:T(2,128)(2,1)S(1)} %all_to_all.10.refs_0_.rows_ref, bf16[1,2,3072]{2,1,0:T(2,128)(2,1)S(1)} %copy-done, f32[1,3072]{1,0:T(1,128)S(1)} %get-tuple-element.15.refs_2_.gain_ref), custom_call_target="tpu_custom_call" | custom-call | tf_op jit(solution)/shard_map/finish/pallas_call | solution.py:335
Async XLA Ops:
  18.9 2.0 %collective-permute-start = (bf16[16,2,3072]{2,1,0:T(2,128)(2,1)S(1)}, bf16[16,2,3072]{2,1,0:T(2,128)(2,1)S(1)}, u32[]{:S(2)}, u32[]{:S(2)}) collective-permute-start(bf16[16,2,3072]{2,1,0:T(2,128)(2,1)S(1)} %all_to_all.10.refs_0_.rows_ref), channel_id=1, source_target_pairs={{0,4},{4,0},{1,5},{5,1},{2,6},{6,2},{3,7},{7,3},{8,12},{12,8},{9,1... | collective-permute-start | bytes 589832 | tf_op jit(solution)/shard_map/ppermute | solution.py:265
  20.9 26.8 %copy-start = (bf16[1,2,3072]{2,1,0:T(2,128)(2,1)S(1)}, bf16[1,2,3072]{2,1,0:T(2,128)(2,1)}, u32[]{:S(2)}) copy-start(bf16[1,2,3072]{2,1,0:T(2,128)(2,1)} %saved_ref.3) | copy-start | bytes 36868
  33.6 14.1 %all-to-all-start.1 = ((bf16[8,4,3072]{2,1,0:T(4,128)(2,1)}), bf16[8,4,3072]{2,1,0:T(4,128)(2,1)S(1)}, u32[]{:S(2)}, u32[]{:S(2)}) async-start(bf16[8,4,3072]{2,1,0:T(4,128)(2,1)} %get-tuple-element.18), calls=%async_computation.1 | async-start | bytes 393216 | tf_op jit(solution)/shard_map/all_to_all | solution.py:314
  37.2 1.5 %collective-permute-start.1 = (bf16[2,16,2048]{2,1,0:T(8,128)(2,1)S(1)}, bf16[2,16,2048]{2,1,0:T(8,128)(2,1)S(1)}, u32[]{:S(2)}, u32[]{:S(2)}) collective-permute-start(bf16[2,16,2048]{2,1,0:T(8,128)(2,1)S(1)} %get-tuple-element.23.refs_0_), channel_id=1, source_target_pairs={{0,4},{4,0},{1,5},{5,1},{2,6},{6,2},{3,7},{7,3},{8,12},{12,8},{9,1... | collective-permute-start | bytes 393224 | tf_op jit(solution)/shard_map/ppermute | solution.py:312

commit v7 on v6

--- a/solution.py
+++ b/solution.py
@@ -53,7 +53,7 @@
 
     def spread(source, target, sem):
         def start(lane, carry):
-            pltpu.make_async_copy(source, sent_ref.at[target * mp + lane], sems.at[sem]).start()
+            pltpu.make_async_copy(source, sent_ref.at[lane, target], sems.at[sem]).start()
             return carry
 
         lax.fori_loop(0, mp, start, 0, unroll=mp <= 8)
@@ -77,7 +77,7 @@
         spread(grad_ref.at[0], behind, 2)
 
     for sem in range(3):
-        whole = sent_ref.at[pl.ds(0, mp)]
+        whole = sent_ref.at[:, 0]
         pltpu.make_async_copy(whole, whole, sems.at[sem]).wait()
 
 
@@ -101,8 +101,7 @@
     hid_ref, part_ref, norm_ref, up_ref = refs[dp + 5 : dp + 9]
     both, win, wout, branch, dnorm, sem_in, sem_out = refs[dp + 9 :]
     section, replica = lax.axis_index("section"), lax.axis_index("dp")
-    lanes = rows_refs[0].shape[0] // sections
-    block = lanes * rows_refs[0].shape[1]
+    block = rows_refs[0].shape[0] * rows_refs[0].shape[2]
     tokens = dp * block
     width = win_first.shape[1]
     hidden = chunks * width
@@ -125,11 +124,10 @@
     gain = gain_ref[...]
 
     def rows_of(slot, owner):
-        here = pl.ds(slot * lanes, lanes)
-        rows = rows_refs[0][here]
+        rows = rows_refs[0][:, slot]
         for k in range(1, dp):
             rows = jnp.where(
-                lax.rem(replica + dp - k, dp) == owner, rows_refs[k][here], rows
+                lax.rem(replica + dp - k, dp) == owner, rows_refs[k][:, slot], rows
             )
         return rows.reshape(block, rows.shape[-1])
 
@@ -217,16 +215,16 @@
         copy.wait()
 
 
-def finish_kernel(sections, mp, recv_ref, rows_ref, saved_ref, gain_ref, act_ref, grad_ref):
+def finish_kernel(sections, recv_ref, rows_ref, saved_ref, gain_ref, act_ref, grad_ref):
     section, lane = lax.axis_index("section"), lax.axis_index("mp")
     mine = saved_ref.shape[1]
     total = jnp.sum(recv_ref[...].astype(F32), axis=0)
-    behind = lax.rem(section + sections - 1, sections) * mp + lane
-    ahead = lax.rem(section + 1, sections) * mp + lane
-    act_ref[0] = (rows_ref[behind].astype(F32) + total[:mine]).astype(BF16)
+    behind = lax.rem(section + sections - 1, sections)
+    ahead = lax.rem(section + 1, sections)
+    act_ref[0] = (rows_ref[lane, behind].astype(F32) + total[:mine]).astype(BF16)
     nhat, rstd = normalize(saved_ref[0].astype(F32))
     scaled = total[mine:] * gain_ref[...]
-    grad = rows_ref[ahead].astype(F32) + rstd * (
+    grad = rows_ref[lane, ahead].astype(F32) + rstd * (
         scaled
         - jnp.mean(scaled, axis=-1, keepdims=True)
         - nhat * jnp.mean(scaled * nhat, axis=-1, keepdims=True)
@@ -253,12 +251,13 @@
         functools.partial(send_kernel, sections, mp),
         in_specs=[hbm] * 5,
         out_specs=vmem,
-        out_shape=like((sections * mp, mine, width), BF16),
+        out_shape=like((mp, sections, mine, width), BF16),
         scratch_shapes=[pltpu.SemaphoreType.DMA((3,))],
         compiler_params=params(4),
         name="send",
     )(*stay(act_sent, new_batch, saved_input, grad_sent, loss_grad))
-    got = lax.all_to_all(sent, ("section", "mp"), 0, 0)
+    got = lax.all_to_all(sent.reshape(mp * sections, mine, width), ("mp", "section"), 0, 0)
+    got = got.reshape(mp, sections, mine, width)
     chunks = divisor(hidden // 128, 8)
     first = hidden // chunks
     rows = [got] + [
@@ -333,7 +332,7 @@
     )(n_bwd, upstream, *hids)
 
     act_out, grad_out = pl.pallas_call(
-        functools.partial(finish_kernel, sections, mp),
+        functools.partial(finish_kernel, sections),
         in_specs=[vmem] * 4,
         out_specs=[vmem] * 2,
         out_shape=[like((1, mine, width), BF16)] * 2,

time: 49 us -> 48.5 us (0.990)
  blocking collectives: 17.4 us -> 16.9 us
    all_to_all x1, blocking collectives: 17.4 us -> 16.9 us  [per_device(): lax.all_to_all(sent.reshape(mp * sections, mine, width), ('mp', 'section'...]
  transfers between devices with their start and end apart: 3 -> 3, of which waited for: 1 -> 1; matrix products, arithmetic and copies ran while one was open for 0% -> 0% of each run, Pallas kernels for 22% -> 23%
where the time goes in v7:
time: 48.5 us; the launch traced here: 48.2 us
  Pallas kernels  25.5 us (53%)
  blocking collectives  16.9 us (35%)
  starting transfers between devices  4.11 us (8%)
  waiting for transfers between devices  1.02 us (2%)
  between operations  0.71 us (1%)
    all_to_all x1, blocking collectives, per_device(): lax.all_to_all(sent.reshape(mp * sections, mine, width), ('mp', 'section'...  16.9 us
    pallas_call x1, Pallas kernels, per_device(): pl.pallas_call(functools.partial(block_kernel, sections, dp, chunks, 3),...  12.6 us
    pallas_call x1, Pallas kernels, per_device(): pl.pallas_call(functools.partial(weight_kernel, dp, tile), in_specs=[vmem...  9.01 us
    all_to_all x1, starting transfers between devices, per_device(): recv = lax.all_to_all(part, ('dp', 'mp'), 0, 0)  3.58 us
    pallas_call x1, Pallas kernels, per_device(): pl.pallas_call(functools.partial(early_kernel, dp), in_specs=[hbm] * 3, o...  1.94 us
    ppermute x1, waiting for transfers between devices, per_device(): lax.ppermute(hid, 'dp', [(i, (i + k) % dp) for i in range(dp)])  1.01 us
  transfers between devices with their start and end apart: 3, of which 1 were waited for; matrix products, arithmetic and copies ran while one was open for 0% of the time, Pallas kernels for 23%

profile of v7, /device:TPU:0, one launch (start us, length us, event | category | flops | bytes accessed | tf_op | source)
XLA Modules:
  0.0 48.2 jit_solution(2879073534720584973)
XLA Ops:
  0.6 0.9 %send.1 = bf16[4,4,2,3072]{3,2,1,0:T(2,128)(2,1)S(1)} custom-call(bf16[1,2,3072]{2,1,0:T(2,128)(2,1)} %act_ref.1, bf16[2,3072]{1,0:T(2,128)(2,1)} %batch_ref.1, bf16[1,2,3072]{2,1,0:T(2,128)(2,1)} %saved_ref.3, bf16[1,2,3072]{2,1,0:T(2,128)(2,1)} %grad_ref.1, bf16[2,3072]{1,0:T(2,128)(2,1)} %loss_ref.1), custom_call_target="tpu_custom_call" | custom-call | tf_op jit(solution)/shard_map/send/pallas_call | solution.py:250
  1.5 16.9 %all_to_all.10 = bf16[16,2,3072]{2,1,0:T(2,128)(2,1)S(1)} all-to-all(bf16[16,2,3072]{2,1,0:T(2,128)(2,1)S(1)} %bitcast.9), channel_id=1, replica_groups=mesh['section'=4,'dp'=2,'mp'=4] {'mp','section'}, dimensions={0} | all-to-all | bytes 393216 | tf_op jit(solution)/shard_map/all_to_all | solution.py:259
  18.4 0.0 collective-permute-start
  18.4 1.9 %early.1 = (f32[1,3072]{1,0:T(1,128)S(1)}, bf16[3072,256]{1,0:T(8,128)(2,1)S(1)}, bf16[3072,256]{1,0:T(8,128)(2,1)S(1)}) custom-call(f32[1,3072]{1,0:T(1,128)} %gain_hbm.1, bf16[3072,4096]{1,0:T(8,128)(2,1)} %bitcast.10, bf16[3072,4096]{1,0:T(8,128)(2,1)} %bitcast.12), custom_call_target="tpu_custom_call" | custom-call | bytes 3145728 | tf_op jit(solution)/shard_map/early/pallas_call | solution.py:266
  20.4 0.0 collective-permute-done.refs_1_
  20.4 0.0 copy-start
  20.4 12.6 %block.1 = (bf16[2,16,2048]{2,1,0:T(8,128)(2,1)S(1)}, bf16[8,4,3072]{2,1,0:T(4,128)(2,1)}, bf16[16,3072]{1,0:T(8,128)(2,1)S(1)}, bf16[16,3072]{1,0:T(8,128)(2,1)S(1)}) custom-call(bf16[4,4,2,3072]{3,2,1,0:T(2,128)(2,1)S(1)} %bitcast.7, bf16[4,4,2,3072]{3,2,1,0:T(2,128)(2,1)S(1)} %collective-permute-done.refs_1_, ...), custom_call_target="tpu_custom_call" | custom-call | flops 1207959552 | bytes 25165824 | tf_op jit(solution)/shard_map/block/pallas_call | solution.py:284
  33.0 3.6 %all-to-all-start.1 = ((bf16[8,4,3072]{2,1,0:T(4,128)(2,1)}), bf16[8,4,3072]{2,1,0:T(4,128)(2,1)S(1)}, u32[]{:S(2)}, u32[]{:S(2)}) async-start(bf16[8,4,3072]{2,1,0:T(4,128)(2,1)} %get-tuple-element.18), calls=%async_computation.1 | async-start | bytes 393216 | tf_op jit(solution)/shard_map/all_to_all | solution.py:313
  36.6 0.5 %collective-permute-start.1 = (bf16[2,16,2048]{2,1,0:T(8,128)(2,1)S(1)}, bf16[2,16,2048]{2,1,0:T(8,128)(2,1)S(1)}, u32[]{:S(2)}, u32[]{:S(2)}) collective-permute-start(bf16[2,16,2048]{2,1,0:T(8,128)(2,1)S(1)} %get-tuple-element.23.refs_0_), channel_id=1, source_target_pairs={{0,4},{4,0},{1,5},{5,1},{2,6},{6,2},{3,7},{7,3},{8,12},{12,8},{9,1... | collective-permute-start | bytes 393224 | tf_op jit(solution)/shard_map/ppermute | solution.py:311
  37.2 1.0 %collective-permute-done.1.refs_1_ = bf16[2,16,2048]{2,1,0:T(8,128)(2,1)S(1)} collective-permute-done((bf16[2,16,2048]{2,1,0:T(8,128)(2,1)S(1)}, bf16[2,16,2048]{2,1,0:T(8,128)(2,1)S(1)}, u32[]{:S(2)}, u32[]{:S(2)}) %collective-permute-start.1) | collective-permute-done | bytes 131104 | tf_op jit(solution)/shard_map/ppermute | solution.py:311
  38.2 9.0 %weight.1 = (bf16[1536,4096]{1,0:T(8,128)(2,1)}, bf16[1536,4096]{1,0:T(8,128)(2,1)}) custom-call(bf16[16,3072]{1,0:T(8,128)(2,1)S(1)} %get-tuple-element.21.norm_ref, bf16[16,3072]{1,0:T(8,128)(2,1)S(1)} %get-tuple-element.22.up_ref, bf16[2,16,2048]{2,1,0:T(8,128)(2,1)S(1)} %get-tuple-element.23.refs_0_, bf16[2,16,2048]{2,1,0:T(8,128)(2,1)S(1)} %collective-permute-done.1.refs_1_), custom_call_target="tpu_custom_call" | custom-call | flops 402653184 | bytes 25165824 | tf_op jit(solution)/shard_map/weight/pallas_call | solution.py:317
  47.2 0.0 all-to-all-done.1.recv_ref
  47.2 0.0 copy-done
  47.2 1.0 %finish.1 = (bf16[1,2,3072]{2,1,0:T(2,128)(2,1)}, bf16[1,2,3072]{2,1,0:T(2,128)(2,1)}) custom-call(bf16[8,4,3072]{2,1,0:T(4,128)(2,1)S(1)} %all-to-all-done.1.recv_ref, bf16[4,4,2,3072]{3,2,1,0:T(2,128)(2,1)S(1)} %bitcast.8, bf16[1,2,3072]{2,1,0:T(2,128)(2,1)S(1)} %copy-done, f32[1,3072]{1,0:T(1,128)S(1)} %get-tuple-element.15.refs_2_.gain_ref), custom_call_target="tpu_custom_call" | custom-call | tf_op jit(solution)/shard_map/finish/pallas_call | solution.py:334
Async XLA Ops:
  18.4 2.0 %collective-permute-start = (bf16[4,4,2,3072]{3,2,1,0:T(2,128)(2,1)S(1)}, bf16[4,4,2,3072]{3,2,1,0:T(2,128)(2,1)S(1)}, u32[]{:S(2)}, u32[]{:S(2)}) collective-permute-start(bf16[4,4,2,3072]{3,2,1,0:T(2,128)(2,1)S(1)} %bitcast.6), channel_id=1, source_target_pairs={{0,4},{4,0},{1,5},{5,1},{2,6},{6,2},{3,7},{7,3},{8,12},{12,8},{9,1... | collective-permute-start | bytes 589832 | tf_op jit(solution)/shard_map/ppermute | solution.py:264
  20.4 26.8 %copy-start = (bf16[1,2,3072]{2,1,0:T(2,128)(2,1)S(1)}, bf16[1,2,3072]{2,1,0:T(2,128)(2,1)}, u32[]{:S(2)}) copy-start(bf16[1,2,3072]{2,1,0:T(2,128)(2,1)} %saved_ref.3) | copy-start | bytes 36868
  33.0 14.1 %all-to-all-start.1 = ((bf16[8,4,3072]{2,1,0:T(4,128)(2,1)}), bf16[8,4,3072]{2,1,0:T(4,128)(2,1)S(1)}, u32[]{:S(2)}, u32[]{:S(2)}) async-start(bf16[8,4,3072]{2,1,0:T(4,128)(2,1)} %get-tuple-element.18), calls=%async_computation.1 | async-start | bytes 393216 | tf_op jit(solution)/shard_map/all_to_all | solution.py:313
  36.6 1.5 %collective-permute-start.1 = (bf16[2,16,2048]{2,1,0:T(8,128)(2,1)S(1)}, bf16[2,16,2048]{2,1,0:T(8,128)(2,1)S(1)}, u32[]{:S(2)}, u32[]{:S(2)}) collective-permute-start(bf16[2,16,2048]{2,1,0:T(8,128)(2,1)S(1)} %get-tuple-element.23.refs_0_), channel_id=1, source_target_pairs={{0,4},{4,0},{1,5},{5,1},{2,6},{6,2},{3,7},{7,3},{8,12},{12,8},{9,1... | collective-permute-start | bytes 393224 | tf_op jit(solution)/shard_map/ppermute | solution.py:311
